TPU v7x, 256 devices: a whole 4x4x8 slice. The times are simulated.
256 devices in a mesh: frame: 32 (over z_hi, y, core), head: 8 (over z_lo, x).
Axes of the slice: x: 4, y: 4, z: 8 (z_hi: 4, z_lo: 2; z = z_hi * 2 + z_lo), core: 2. Of those that a mesh axis runs over, the one named last changes fastest.
Arguments:
- tokens: bfloat16 [8192, 3072], P('frame'), may hold values from -6 to 6
- w_qkv: bfloat16 [3, 3072, 3072], P(None, None, 'head'), may hold values from -0.109375 to 0.109375
- norm_gains: float32 [2, 3072], P(None, 'head'), may hold values from 0.8 to 2.5
- w_out: bfloat16 [3072, 3072], P('head'), may hold values from -0.15625 to 0.15625
- near_mask: int32 [64, 4], P('frame'), may hold values 0 or 1
- far_pattern: int32 [64, 64], P('frame'), may hold values from 0 to 1, as said below
- window: int32 [32], replicated, may hold values from 1 to 256, as said below
Outputs:
- layer_out: bfloat16 [8192, 3072], P('frame', 'head')
- checksum: float32 [8192], P('frame')
Inputs may be any that keep to these rules, and one draw needn't show every extreme that they name: `far_pattern`: 0 or 1; entries whose two blocks lie in slabs less than two apart are never read. Entry d is the window for slabs d apart; entry 0 is 256.
All inputs are finite; a program needn't handle non-finite values. No bound on the sum of `near_mask` on one device may be relied on, other than what follows from the above.
Results may differ from a plain program's by a relative error of at most 0.015.
Values may be sent and summed in bfloat16 or wider, within the bound.
A program may use at most 128 MiB of HBM per device.

v0:
```python
import jax
import jax.numpy as jnp
from jax import lax
from jax.sharding import PartitionSpec as P

D = 3072
HD = 128
BLK = 128


def with_halo(cells, sides, width):
    for axis, dim in sides:
        count = lax.axis_size(axis)
        ends = count - 1
        head = lax.slice_in_dim(cells, 0, width, axis=dim)
        tail = lax.slice_in_dim(cells, cells.shape[dim] - width, cells.shape[dim], axis=dim)
        cells = jnp.concatenate(
            [
                lax.ppermute(tail, axis, [(i, (i + 1) % count) for i in range(ends)]),
                cells,
                lax.ppermute(head, axis, [((i + 1) % count, i) for i in range(ends)]),
            ],
            axis=dim,
        )
    return cells


def normed_heads(values, gain_row):
    shaped = values.reshape(values.shape[0], -1, HD)
    factor = lax.rsqrt(jnp.mean(shaped * shaped, axis=-1, keepdims=True) + 1e-06)
    return shaped * factor * gain_row.reshape(-1, HD)


def lookup_columns(table_int, columns, table_width):
    onehot = (jnp.arange(table_width, dtype=jnp.int32)[:, None] == columns[None, :]).astype(
        jnp.float32
    )
    return jnp.dot(table_int.astype(jnp.float32), onehot)


def attend(totals, key_part, value_part, first_row, context, which_keys):
    queries, near_mask, far_pattern, window, frame_id, slab_rows, n_frame = context
    numer, denom = totals
    key_span = key_part.shape[0]
    n_blocks = near_mask.shape[0]
    key_index = first_row + jnp.arange(key_span, dtype=jnp.int32)
    key_slab = key_index // slab_rows
    key_pos = key_index % slab_rows
    distance = jnp.abs(key_slab - frame_id)
    far_sel = lookup_columns(far_pattern, key_index // BLK, far_pattern.shape[1])
    key_side = jnp.where(key_slab < frame_id, 0, 1)
    near_sel = lookup_columns(near_mask, key_side * n_blocks + key_pos // BLK, 2 * n_blocks)
    if which_keys == "near":
        chosen = jnp.where(distance == 0, 1.0, jnp.where(distance == 1, near_sel, 0.0))
    else:
        chosen = jnp.where(distance >= 2, far_sel, 0.0)
    chosen = jnp.broadcast_to(chosen[:, None, :], (n_blocks, BLK, key_span)).reshape(
        slab_rows, key_span
    )
    inside = (key_index >= 0) & (key_index < slab_rows * n_frame)
    slab_steps = jnp.arange(n_frame, dtype=jnp.int32)
    key_limit = jnp.sum(
        jnp.where(slab_steps[:, None] == distance[None, :], window[:, None], 0), axis=0
    )
    position = jnp.arange(slab_rows, dtype=jnp.int32)
    allowed = (
        (chosen > 0.5)
        & inside[None, :]
        & (jnp.abs(position[:, None] - key_pos[None, :]) < key_limit[None, :])
    )
    key_heads = key_part.reshape(key_span, -1, HD)
    value_heads = value_part.reshape(key_span, -1, HD)
    scores = jnp.einsum("qhd,khd->hqk", queries, key_heads, preferred_element_type=jnp.float32)
    weights = jnp.where(allowed[None], jnp.exp(scores), 0.0)
    numer = numer + jnp.einsum(
        "hqk,khd->qhd",
        weights.astype(jnp.bfloat16),
        value_heads,
        preferred_element_type=jnp.float32,
    )
    denom = denom + jnp.sum(weights, axis=-1)
    return (numer, denom)


def per_device(tokens, w_qkv, norm_gains, w_out, near_mask, far_pattern, window):
    slab_rows = tokens.shape[0]
    frame_id = lax.axis_index("frame")
    n_frame = lax.axis_size("frame")
    query = jnp.dot(tokens, w_qkv[0], preferred_element_type=jnp.float32)
    key_full = jnp.dot(tokens, w_qkv[1], preferred_element_type=jnp.float32)
    value_full = jnp.dot(tokens, w_qkv[2], preferred_element_type=jnp.float32)
    queries = (normed_heads(query, norm_gains[0]) * HD ** (-0.5)).astype(jnp.bfloat16)
    keys_flat = normed_heads(key_full, norm_gains[1]).astype(jnp.bfloat16).reshape(slab_rows, -1)
    values_flat = value_full.astype(jnp.bfloat16)
    head_count = queries.shape[1]
    context = (queries, near_mask, far_pattern, window, frame_id, slab_rows, n_frame)
    start_totals = (
        jnp.zeros((slab_rows, head_count, HD), jnp.float32),
        jnp.zeros((head_count, slab_rows), jnp.float32),
    )
    stacked = jnp.stack([keys_flat, values_flat])
    widened = with_halo(stacked, (("frame", 1),), slab_rows)
    totals = attend(
        start_totals, widened[0], widened[1], (frame_id - 1) * slab_rows, context, "near"
    )
    totals = attend(
        totals,
        lax.all_gather(keys_flat, "frame", axis=0, tiled=True),
        lax.all_gather(values_flat, "frame", axis=0, tiled=True),
        jnp.int32(0),
        context,
        "far",
    )
    numer, denom = totals
    attended = (numer / denom.T[:, :, None]).reshape(slab_rows, -1).astype(jnp.bfloat16)
    full_cols = lax.psum_scatter(
        lax.dot_general(
            w_out, attended, (((0,), (1,)), ((), ())), preferred_element_type=jnp.float32
        ).astype(jnp.bfloat16),
        "head",
        scatter_dimension=0,
        tiled=True,
    ).astype(jnp.float32)
    full_rows = full_cols.T
    layer_out = full_rows.astype(jnp.bfloat16)
    checksum = lax.psum(jnp.sum(full_rows, axis=1) * D ** (-0.5), "head")
    return (layer_out, checksum)


def solution(mesh):
    in_specs = (
        P("frame", None),
        P(None, None, "head"),
        P(None, "head"),
        P("head", None),
        P("frame", None),
        P("frame", None),
        P(),
    )
    out_specs = (P("frame", "head"), P("frame"))
    return jax.shard_map(
        per_device, mesh=mesh, in_specs=in_specs, out_specs=out_specs, check_vma=False
    )
```

profile of v0, /device:TPU:2, one launch (start us, length us, event | category | flops | bytes accessed | tf_op | source)
XLA Modules:
  0.0 266.3 jit_solution(1134250349421031782)
XLA Ops:
  7.2 0.0 copy-start
  7.2 0.0 all-gather.5.cloned.1.call-start
  7.2 5.1 %slice_bitcast_fusion = (bf16[384,3072]{0,1:T(8,128)(2,1)}, bf16[384,3072]{0,1:T(8,128)(2,1)}) fusion(bf16[3,3072,384]{2,1,0:T(8,128)(2,1)} %param.8), kind=kLoop, calls=%fused_computation.17 | loop fusion | bytes 9437184 | tf_op jit(solution)/shard_map/dot_general | solution.py:89
  12.4 4.3 %copy.37 = bf16[384,3072]{1,0:T(8,128)(2,1)} copy(bf16[384,3072]{0,1:T(8,128)(2,1)} %get-tuple-element.5) | data formatting | bytes 4718592 | tf_op jit(solution)/shard_map/dot_general | solution.py:90
  16.6 0.0 copy-done.8
  16.7 3.0 %multiply_reduce_fusion.1 = (f32[256,3]{0,1:T(4,128)S(1)}, f32[256,3,128]{0,2,1:T(8,128)S(1)}) fusion(bf16[3,128,3072]{2,1,0:T(8,128)(2,1)} %bitcast.69, bf16[256,3072]{1,0:T(8,128)(2,1)} %param.7), kind=kOutput, calls=%fused_computation.50 | convolution fusion | flops 604175616 | bytes 4328448 | tf_op jit(solution)/shard_map/dot_general | solution.py:90
  19.6 0.8 multiply_convert_fusion.1
  20.4 0.0 all-gather.5.cloned.1.call-update
  20.5 0.0 all-gather.3.cloned.1.call-start
  20.5 3.8 %fusion.27 = bf16[256,384]{1,0:T(8,128)(2,1)} fusion(bf16[256,3072]{1,0:T(8,128)(2,1)} %param.7, bf16[3,3072,384]{2,1,0:T(8,128)(2,1)} %param.8), kind=kOutput, calls=%fused_computation.34 | convolution fusion | flops 604078080 | bytes 4128768 | tf_op jit(solution)/shard_map/dot_general | solution.py:91
  24.4 0.0 all-gather.3.cloned.1.call-update
  24.4 0.0 reduce-scatter.4.cloned.1.call-start
  24.4 0.2 copy.38
  24.6 1.7 pad_maximum_fusion.1
  26.3 1.3 collective-permute-start.1
  27.6 3.2 %collective-permute-start = (bf16[2,256,384]{2,1,0:T(8,128)(2,1)}, bf16[2,256,384]{2,1,0:T(8,128)(2,1)S(1)}, u32[]{:S(2)}, u32[]{:S(2)}) collective-permute-start(bf16[2,256,384]{2,1,0:T(8,128)(2,1)} %pad_maximum_fusion.1), channel_id=1, source_target_pairs={{0,8},{8,16},{16,24},{24,32},{32,40},{40,48},{48,56},{56,64},{64,7... | collective-permute-start | bytes 1179656 | tf_op jit(solution)/shard_map/ppermute | solution.py:19
  30.9 0.0 copy-start.9
  30.9 0.0 copy-start.10
  30.9 4.3 %copy.40 = bf16[384,3072]{1,0:T(8,128)(2,1)} copy(bf16[384,3072]{0,1:T(8,128)(2,1)} %get-tuple-element.4) | data formatting | bytes 4718592 | tf_op jit(solution)/shard_map/dot_general | solution.py:89
  35.3 0.2 select_reduce_fusion
  35.5 0.4 fusion.7
  36.0 3.8 %fusion.8 = pred[256,8192]{1,0:T(8,128)(4,1)} fusion(s32[8192]{0:T(1024)S(1)} %select_reduce_fusion, s32[8192]{0:T(1024)S(1)} %fusion.35, pred[8192]{0:T(1024)(128)(4,1)S(1)} %iota_compare_fusion.4, pred[2,8192]{1,0:T(4,128)(4,1)S(1)} %fusion.7), kind=kLoop, calls=%fused_computation.10 | loop fusion | flops 10485760 | bytes 2187264 | tf_op jit(solution)/shard_map/and | solution.py:67
  39.9 0.1 select_reduce_fusion.1
  40.0 0.0 copy-done.11
  40.0 0.1 fusion.32
  40.1 0.9 fusion.34
  41.0 3.0 %multiply_reduce_fusion = (f32[256,3]{0,1:T(4,128)S(1)}, f32[256,3,128]{0,2,1:T(8,128)}) fusion(bf16[3,128,3072]{2,1,0:T(8,128)(2,1)S(1)} %bitcast.68, bf16[256,3072]{1,0:T(8,128)(2,1)} %param.7), kind=kOutput, calls=%fused_computation.48 | convolution fusion | flops 604175616 | bytes 4328448 | tf_op jit(solution)/shard_map/dot_general | solution.py:89
  44.1 0.0 collective-permute-done.1
  44.1 0.0 collective-permute-done
  44.1 0.1 pad_maximum_fusion
  44.2 0.1 fusion.66
  44.4 1.1 copy.39
  45.4 0.3 copy.41
  45.7 3.2 %fusion.13 = (f32[3,256]{1,0:T(4,128)S(1)}, f32[3,256,768]{2,1,0:T(8,128)}) fusion(pred[256,768]{1,0:T(8,128)(4,1)} %fusion.34, bf16[768,3,128]{0,2,1:T(8,128)(2,1)S(1)} %bitcast.70, f32[256,3,128]{0,2,1:T(8,128)} %get-tuple-element.11, f32[3,128]{1,0:T(4,128)S(1)} %bitcast.78, f32[256,3]{0,1:T(4,128)S(1)} %add_rsqrt_fusion), kind=kOutput, calls=%fused_computation.21 | convolution fusion | flops 152567040 | bytes 3546624 | tf_op jit(solution)/shard_map/qhd,khd->hqk/dot_general | solution.py:73
  48.9 50.5 %all-gather.5.cloned.1.call-done = bf16[8192,384]{0,1:T(8,128)(2,1)} async-done(((bf16[256,384]{0,1:T(8,128)(2,1)}), bf16[8192,384]{0,1:T(8,128)(2,1)}) %all-gather.5.cloned.1.call-update) | async-done | bytes 6291472 | tf_op jit(solution)/shard_map/all_gather | solution.py:108
  99.5 14.9 %fusion = (f32[3,256]{1,0:T(4,128)S(1)}, f32[3,256,8192]{2,1,0:T(8,128)}) fusion(pred[256,8192]{1,0:T(8,128)(4,1)} %fusion.8, bf16[8192,3,128]{0,2,1:T(8,128)(2,1)} %bitcast.81, f32[256,3,128]{0,2,1:T(8,128)S(1)} %copy-done.7, f32[3,128]{1,0:T(4,128)S(1)} %bitcast.79, f32[256,3]{0,1:T(4,128)S(1)} %add_rsqrt_fusion), kind=kOutput, calls=%fused_computation.1 | convolution fusion | flops 1623588096 | bytes 33955328 | tf_op jit(solution)/shard_map/qhd,khd->hqk/dot_general | solution.py:73
  114.3 56.0 %all-gather.3.cloned.1.call-done = bf16[8192,384]{1,0:T(8,128)(2,1)} async-done(((bf16[256,384]{1,0:T(8,128)(2,1)}), bf16[8192,384]{1,0:T(8,128)(2,1)}) %all-gather.3.cloned.1.call-update) | async-done | bytes 6291472 | tf_op jit(solution)/shard_map/all_gather | solution.py:109
  170.3 8.5 %copy.44 = bf16[8192,384]{0,1:T(8,128)(2,1)} copy(bf16[8192,384]{1,0:T(8,128)(2,1)} %all-gather.3.cloned.1.call-done) | data formatting | bytes 12582912 | tf_op jit(solution)/shard_map/all_gather | solution.py:109
  178.9 13.7 %fusion.2 = f32[3,128,256]{2,1,0:T(8,128)} fusion(bf16[8192,3,128]{0,2,1:T(8,128)(2,1)} %bitcast.67, f32[3,256,8192]{2,1,0:T(8,128)} %get-tuple-element.15, pred[256,8192]{1,0:T(8,128)(4,1)} %fusion.8), kind=kOutput, calls=%fused_computation.3 | convolution fusion | flops 1623195648 | bytes 33947648 | tf_op jit(solution)/shard_map/hqk,khd->qhd/dot_general | solution.py:75
  192.6 2.3 fusion.24
  194.9 2.2 fusion.9
  197.0 2.6 copy.51
  199.6 0.0 reduce-scatter.4.cloned.1.call-update
  199.6 39.1 %reduce-scatter.4.cloned.1.call-done = bf16[384,256]{1,0:T(8,128)(2,1)} async-done(((bf16[3072,256]{1,0:T(8,128)(2,1)}), bf16[384,256]{1,0:T(8,128)(2,1)}) %reduce-scatter.4.cloned.1.call-update) | async-done | bytes 196624
  238.7 1.1 copy.52
  239.8 0.0 copy-start.5
  239.8 0.1 convert_reduce_fusion
  239.9 19.8 %psum.7 = f32[256]{0:T(256)} all-reduce(f32[256]{0:T(256)S(1)} %broadcast_multiply_fusion), channel_id=1, replica_groups=mesh['frame'=32,'head'=8] {'head'}, use_global_device_ids=true, to_apply=%region_8.9 | all-reduce | flops 256 | bytes 2048 | tf_op jit(solution)/shard_map/psum | solution.py:126
  (32 shorter events, 0.2 us)
Async XLA Ops:
  7.2 187.7 %copy-start = (bf16[384,3072]{1,0:T(8,128)(2,1)S(1)}, bf16[384,3072]{1,0:T(8,128)(2,1)}, u32[]{:S(2)}) copy-start(bf16[384,3072]{1,0:T(8,128)(2,1)} %param.10) | copy-start | bytes 7077892
  7.2 92.3 %all-gather.5.cloned.1.call-start = ((), (), s32[]{:S(2)}) async-start(), calls=%async_computation.2 | async-start | bytes 6488064 | tf_op jit(solution)/shard_map/all_gather | solution.py:108
  12.3 4.3 %copy-start.8 = (f32[2,384]{1,0:T(2,128)S(1)}, f32[2,384]{1,0:T(2,128)}, u32[]{:S(2)}) copy-start(f32[2,384]{1,0:T(2,128)} %param.9) | copy-start | bytes 9220
  20.5 4.0 %copy-start.3 = (bf16[256,3,128]{0,2,1:T(8,128)(2,1)S(1)}, bf16[256,3,128]{0,2,1:T(8,128)(2,1)}, u32[]{:S(2)}) copy-start(bf16[256,3,128]{0,2,1:T(8,128)(2,1)} %multiply_convert_fusion.1) | copy-start | bytes 589828
  20.5 149.9 %all-gather.3.cloned.1.call-start = ((), (), s32[]{:S(2)}) async-start(), calls=%async_computation.1 | async-start | bytes 6488064 | tf_op jit(solution)/shard_map/all_gather | solution.py:109
  24.4 214.3 %reduce-scatter.4.cloned.1.call-start = ((), (), s32[]{:S(2)}) async-start(), calls=%async_computation.3 | async-start | bytes 1769472
  26.3 17.7 %collective-permute-start.1 = (bf16[2,256,384]{2,1,0:T(8,128)(2,1)}, bf16[2,256,384]{2,1,0:T(8,128)(2,1)S(1)}, u32[]{:S(2)}, u32[]{:S(2)}) collective-permute-start(bf16[2,256,384]{2,1,0:T(8,128)(2,1)} %pad_maximum_fusion.1), channel_id=1, source_target_pairs={{8,0},{16,8},{24,16},{32,24},{40,32},{48,40},{56,48},{64,56},{72,6... | collective-permute-start | bytes 1179656 | tf_op jit(solution)/shard_map/ppermute | solution.py:21
  27.6 16.5 %collective-permute-start = (bf16[2,256,384]{2,1,0:T(8,128)(2,1)}, bf16[2,256,384]{2,1,0:T(8,128)(2,1)S(1)}, u32[]{:S(2)}, u32[]{:S(2)}) collective-permute-start(bf16[2,256,384]{2,1,0:T(8,128)(2,1)} %pad_maximum_fusion.1), channel_id=1, source_target_pairs={{0,8},{8,16},{16,24},{24,32},{32,40},{40,48},{48,56},{56,64},{64,7... | collective-permute-start | bytes 1179656 | tf_op jit(solution)/shard_map/ppermute | solution.py:19
  30.9 4.4 %copy-start.9 = (s32[32]{0:T(128)S(1)}, s32[32]{0:T(128)}, u32[]{:S(2)}) copy-start(s32[32]{0:T(128)} %param.13) | copy-start | bytes 388
  30.9 4.6 %copy-start.10 = (s32[2,64]{1,0:T(2,128)S(1)}, s32[2,64]{1,0:T(2,128)}, u32[]{:S(2)}) copy-start(s32[2,64]{1,0:T(2,128)} %param.12) | copy-start | bytes 1540
  35.2 4.8 %copy-start.11 = (s32[2,4]{1,0:T(2,128)S(1)}, s32[2,4]{1,0:T(2,128)}, u32[]{:S(2)}) copy-start(s32[2,4]{1,0:T(2,128)} %param.11) | copy-start | bytes 100
  35.2 5.8 %copy-start.1 = (bf16[384,3072]{1,0:T(8,128)(2,1)S(1)}, bf16[384,3072]{1,0:T(8,128)(2,1)}, u32[]{:S(2)}) copy-start(bf16[384,3072]{1,0:T(8,128)(2,1)} %copy.40) | copy-start | bytes 7077892
  41.0 3.1 %copy-start.2 = (bf16[256,384]{1,0:T(8,128)(2,1)S(1)}, bf16[256,384]{1,0:T(8,128)(2,1)}, u32[]{:S(2)}) copy-start(bf16[256,384]{1,0:T(8,128)(2,1)} %fusion.27) | copy-start | bytes 589828
  45.7 53.8 %copy-start.7 = (f32[256,3,128]{0,2,1:T(8,128)S(1)}, f32[256,3,128]{0,2,1:T(8,128)}, u32[]{:S(2)}) copy-start(f32[256,3,128]{0,2,1:T(8,128)} %get-tuple-element.11) | copy-start | bytes 1179652
  178.9 13.7 %copy-start.4 = (pred[256,768]{1,0:T(8,128)(4,1)S(1)}, pred[256,768]{1,0:T(8,128)(4,1)}, u32[]{:S(2)}) copy-start(pred[256,768]{1,0:T(8,128)(4,1)} %fusion.34) | copy-start | bytes 589828
  178.9 13.7 %copy-start.6 = (bf16[1,768,384]{1,2,0:T(8,128)(2,1)S(1)}, bf16[1,768,384]{1,2,0:T(8,128)(2,1)}, u32[]{:S(2)}) copy-start(bf16[1,768,384]{1,2,0:T(8,128)(2,1)} %copy.39) | copy-start | bytes 1769476
  239.8 20.0 %copy-start.5 = (bf16[384,256]{0,1:T(8,128)(2,1)}, bf16[384,256]{0,1:T(8,128)(2,1)S(1)}, u32[]{:S(2)}) copy-start(bf16[384,256]{0,1:T(8,128)(2,1)S(1)} %copy.52) | copy-start | bytes 589828
Sparse Core Ops, SparseCore 0:
  20.6 78.8 all-gather.4
  102.6 67.7 all-gather.2
  199.8 38.9 reduce-scatter.3
where the time goes:
time: 267 us; the launch traced here: 266 us
  waiting for transfers between devices  146 us (55%)
  matrix products  46.6 us (17%)
  local copies, waits for them, and re-layouts  27.6 us (10%)
  blocking collectives  19.8 us (7%)
  between operations  14 us (5%)
  other arithmetic  7.97 us (3%)
  starting transfers between devices  4.64 us (2%)
    all_gather x1, waiting for transfers between devices, per_device(): lax.all_gather(values_flat, 'frame', axis=0, tiled=True)  56 us
    all_gather x1, waiting for transfers between devices, per_device(): lax.all_gather(keys_flat, 'frame', axis=0, tiled=True)  50.5 us
    unnamed x4, waiting for transfers between devices  39.1 us
    psum x1, blocking collectives, per_device(): checksum = lax.psum(jnp.sum(full_rows, axis=1) * D ** (-0.5), 'head')  19.8 us
    dot_general x2, matrix products, attend(): jnp.einsum('qhd,khd->hqk', queries, key_heads, preferred_element_type=jnp...  18.1 us
    dot_general x2, matrix products, attend(): jnp.einsum('hqk,khd->qhd', weights.astype(jnp.bfloat16), value_heads, pre...  16 us
    dot_general x2, local copies, waits for them, and re-layouts, per_device(): query = jnp.dot(tokens, w_qkv[0], preferred_element_type=jnp.float32)  9.4 us
    all_gather x1, local copies, waits for them, and re-layouts, per_device(): lax.all_gather(values_flat, 'frame', axis=0, tiled=True)  8.53 us
  transfers between devices with their start and end apart: 5, of which 3 were waited for; matrix products, arithmetic and copies ran while one was open for 14% of the time, Pallas kernels for 0%

commit v1 on v0

v1 whole, which is shorter than its diff:
```python
import jax
import jax.numpy as jnp
from jax import lax
from jax.experimental import pallas as pl
from jax.experimental.pallas import tpu as pltpu
from jax.sharding import PartitionSpec as P

D = 3072
HD = 128
BLK = 128
SLAB = 256
HL = 3
COLS = HL * HD
MESH = pl.DeviceIdType.MESH
BF = jnp.bfloat16
F32 = jnp.float32
LOG2E = 1.4426950408889634
OROWS = BLK + 16
CUT = 80
NT = (((1,), (1,)), ((), ()))


def layer_kernel(
    tok_hbm,
    w_hbm,
    wo_hbm,
    gains_ref,
    thr_ref,
    out_ref,
    cs_ref,
    tok,
    wkv,
    wq,
    wo,
    kv,
    qb,
    tbuf,
    texp,
    dist,
    pbuf,
    num,
    tot,
    osend,
    orel_a,
    orel_b,
    ofin,
    xf,
    xopp,
    xrel,
    xs,
    xfin,
    zs,
    zr,
    csb,
    lsem,
    kss,
    krs,
    qss,
    qrs,
    tss,
    trs,
    oss,
    ors,
    xss,
    xrs,
    css,
    crs,
):
    f = lax.axis_index("frame")
    g = lax.axis_index("head")
    zh, y, c = f // 8, (f // 2) % 4, f % 2
    zl, x = g // 4, g % 4

    def at_y(step):
        return (zh * 8 + ((y + step) % 4) * 2 + c, g)

    def at_z(step):
        return (((zh + step) % 4) * 8 + y * 2 + c, g)

    def at_x(step):
        return (f, zl * 4 + (x + step) % 4)

    core = (zh * 8 + y * 2 + (1 - c), g)
    zlo = (f, (1 - zl) * 4 + x)

    started = []

    def send(src, dst, ssem, rsem, dev):
        copy = pltpu.make_async_remote_copy(
            src_ref=src, dst_ref=dst, send_sem=ssem, recv_sem=rsem, device_id=dev, device_id_type=MESH
        )
        copy.start()
        started.append(copy)
        return copy

    def fetch(src, dst, i):
        copy = pltpu.make_async_copy(src, dst, lsem.at[i])
        copy.start()
        return copy

    tok_in = fetch(tok_hbm, tok, 0)
    kv_in = []
    for h in range(HL):
        hs = pl.ds(h * HD, HD)
        kv_in.append(
            (
                fetch(w_hbm.at[1, :, hs], wkv.at[h, :, pl.ds(0, HD)], 1 + 2 * h),
                fetch(w_hbm.at[2, :, hs], wkv.at[h, :, pl.ds(HD, HD)], 2 + 2 * h),
            )
        )
        if h == 0:
            q_in = fetch(w_hbm.at[0], wq, 7)
    wo_in = fetch(wo_hbm, wo, 8)

    barrier = pltpu.get_barrier_semaphore()
    peers = [at_y(1), at_y(3), core, at_z(1), at_z(3), at_z(2)]
    peers += [(f, (g + k) % 8) for k in range(1, 8)]
    for peer in peers:
        pl.semaphore_signal(barrier, inc=1, device_id=peer, device_id_type=MESH)

    def make_kv(h):
        for copy in kv_in[h]:
            copy.wait()
        both = jnp.dot(tok[...], wkv[h], preferred_element_type=F32)
        key = both[:, :HD]
        factor = lax.rsqrt(jnp.mean(key * key, axis=1, keepdims=True) + 1e-06)
        gain = gains_ref[1:2, h * HD : (h + 1) * HD]
        kv[h, 0, :, 0:HD] = (key * factor * gain).astype(BF)
        kv[h, 0, :, HD : 2 * HD] = both[:, HD:].astype(BF)

    def make_q():
        q_in.wait()
        whole = jnp.dot(tok[...], wq[...], preferred_element_type=F32)
        for h in range(HL):
            query = whole[:, h * HD : (h + 1) * HD]
            factor = lax.rsqrt(jnp.mean(query * query, axis=1, keepdims=True) + 1e-06)
            gain = gains_ref[0:1, h * HD : (h + 1) * HD] * (HD**-0.5 * LOG2E)
            qb[h, 0] = (query * factor * gain).astype(BF)

    top, low = pl.ds(0, BLK), pl.ds(BLK, BLK)
    kcopy, qcopy = {}, {}

    def send_kv(h):
        own = kv.at[h, 0]
        kcopy[h, "R"] = send(own, kv.at[h, 1], kss.at[h, 0], krs.at[h, 0], at_y(1))
        kcopy[h, "L"] = send(own, kv.at[h, 2], kss.at[h, 1], krs.at[h, 1], at_y(3))
        kcopy[h, "c0"] = send(own, kv.at[h, 4], kss.at[h, 2], krs.at[h, 2], core)

    def relay_kv(h):
        kcopy[h, "R"].wait_recv()
        kcopy[h, "RR"] = send(
            kv.at[h, 1, top], kv.at[h, 3, top], kss.at[h, 3], krs.at[h, 3], at_y(1)
        )
        kcopy[h, "c1"] = send(kv.at[h, 1], kv.at[h, 5], kss.at[h, 4], krs.at[h, 4], core)
        kcopy[h, "L"].wait_recv()
        kcopy[h, "LL"] = send(
            kv.at[h, 2, low], kv.at[h, 3, low], kss.at[h, 5], krs.at[h, 5], at_y(3)
        )
        kcopy[h, "c2"] = send(kv.at[h, 2], kv.at[h, 6], kss.at[h, 6], krs.at[h, 6], core)

    def last_kv(h):
        kcopy[h, "RR"].wait_recv()
        kcopy[h, "LL"].wait_recv()
        kcopy[h, "c3"] = send(kv.at[h, 3], kv.at[h, 7], kss.at[h, 7], krs.at[h, 7], core)

    def arrived_kv(h):
        for name in ("c0", "c1", "c2", "c3"):
            kcopy[h, name].wait_recv()

    def send_q(h):
        own = qb.at[h, 0]
        qcopy[h, "R"] = send(own, qb.at[h, 1], qss.at[h, 0], qrs.at[h, 0], at_z(1))
        qcopy[h, "L"] = send(own, qb.at[h, 2], qss.at[h, 1], qrs.at[h, 1], at_z(3))

    def relay_q(h):
        qcopy[h, "R"].wait_recv()
        qcopy[h, "RR"] = send(
            qb.at[h, 1, top], qb.at[h, 3, top], qss.at[h, 2], qrs.at[h, 2], at_z(1)
        )
        qcopy[h, "L"].wait_recv()
        qcopy[h, "LL"] = send(
            qb.at[h, 2, low], qb.at[h, 3, low], qss.at[h, 3], qrs.at[h, 3], at_z(3)
        )

    def arrived_q(h):
        qcopy[h, "RR"].wait_recv()
        qcopy[h, "LL"].wait_recv()

    tok_in.wait()
    make_kv(0)
    pl.semaphore_wait(barrier, len(peers))
    send_kv(0)
    tcopy = [
        send(thr_ref, tbuf.at[1], tss.at[0], trs.at[0], at_z(1)),
        send(thr_ref, tbuf.at[2], tss.at[1], trs.at[1], at_z(3)),
        send(thr_ref, tbuf.at[3], tss.at[2], trs.at[2], at_z(2)),
    ]
    make_q()
    for h in range(HL):
        send_q(h)
    make_kv(1)
    send_kv(1)
    make_kv(2)
    send_kv(2)

    row = lax.broadcasted_iota(jnp.int32, (BLK, SLAB), 0)
    col = lax.broadcasted_iota(jnp.int32, (BLK, SLAB), 1)
    for rh in range(2):
        dist[rh] = jnp.abs(row + rh * BLK - col).astype(F32)
    tbuf[0] = thr_ref[...]
    for copy in tcopy:
        copy.wait_recv()
    table = tbuf[...].reshape(4 * 8, 128).astype(BF)
    half = (col >= BLK).astype(jnp.int32)
    for j in range(8):
        slab = zh * 8 + ((y + (0, 3, 1, 2)[j % 4]) % 4) * 2 + (c if j < 4 else 1 - c)
        pick = (row == half + slab * 2).astype(F32).astype(BF)
        texp[j] = jnp.dot(table, pick, preferred_element_type=F32)

    for h in range(HL):
        relay_kv(h)
        relay_q(h)
        if h >= 1:
            last_kv(h - 1)

    ocopy = {}

    def attend(s):
        rh, h = s // HL, s % HL
        queries = qb[h, :, rh * BLK : (rh + 1) * BLK, :].reshape(4 * BLK, HD)

        def scores(j, carry):
            raw = lax.dot_general(queries, kv[h, j, :, 0:HD], NT, preferred_element_type=F32)
            away = dist[rh]
            cols = pl.ds(pl.multiple_of(j * SLAB, SLAB), SLAB)
            for q in range(4):
                limit = texp[j, q * 8 + rh : q * 8 + rh + 1, :]
                weight = jnp.where(away < limit, jnp.exp2(raw[q * BLK : (q + 1) * BLK]), 0.0)
                pbuf[q * BLK : (q + 1) * BLK, cols] = weight.astype(BF)
            return carry

        lax.fori_loop(0, 8, scores, 0)
        values = kv[h, :, :, HD : 2 * HD].reshape(8 * SLAB, HD)
        values = jnp.concatenate([values, jnp.ones((8 * SLAB, HD), BF)], axis=1)
        result = jnp.dot(pbuf[...], values, preferred_element_type=F32)
        num[s] = result[:BLK, :HD]
        tot[s] = result[:BLK, HD:]
        for q in (1, 2, 3):
            part = result[q * BLK : (q + 1) * BLK]
            osend[s, q - 1, 0:BLK, :] = part[:, :HD].astype(BF)
            osend[s, q - 1, BLK:OROWS, :] = part[:, HD:].T[0:16].astype(BF)
        first, last = pl.ds(0, CUT), pl.ds(CUT, OROWS - CUT)
        ocopy[s, "RR"] = send(
            osend.at[s, 2, first], orel_a.at[s], oss.at[s, 0], ors.at[s, 0], at_z(1)
        )
        ocopy[s, "LL"] = send(
            osend.at[s, 2, last], orel_b.at[s], oss.at[s, 1], ors.at[s, 1], at_z(3)
        )
        ocopy[s, "R1"] = send(
            osend.at[s, 1, last], ofin.at[s, 0, last], oss.at[s, 2], ors.at[s, 2], at_z(1)
        )
        ocopy[s, "L0"] = send(
            osend.at[s, 0, first], ofin.at[s, 1, first], oss.at[s, 3], ors.at[s, 3], at_z(3)
        )

    def relay_o(s):
        first, last = pl.ds(0, CUT), pl.ds(CUT, OROWS - CUT)
        ocopy[s, "RR"].wait_recv()
        osend[s, 1, 0:CUT, :] = (
            osend[s, 1, 0:CUT, :].astype(F32) + orel_a[s].astype(F32)
        ).astype(BF)
        ocopy[s, "R0"] = send(
            osend.at[s, 1, first], ofin.at[s, 0, first], oss.at[s, 4], ors.at[s, 4], at_z(1)
        )
        ocopy[s, "LL"].wait_recv()
        osend[s, 0, CUT:OROWS, :] = (
            osend[s, 0, CUT:OROWS, :].astype(F32) + orel_b[s].astype(F32)
        ).astype(BF)
        ocopy[s, "L1"] = send(
            osend.at[s, 0, last], ofin.at[s, 1, last], oss.at[s, 5], ors.at[s, 5], at_z(3)
        )

    def attended_of(s):
        for name in ("R0", "R1", "L0", "L1"):
            ocopy[s, name].wait_recv()
        more = ofin[s, 0].astype(F32) + ofin[s, 1].astype(F32)
        numer = num[s] + more[:BLK]
        strip = more[BLK:OROWS]
        total = tot[s] + jnp.concatenate([strip] * 8, axis=0).T
        return (numer / total).astype(BF)

    xcopy, ccopy = {}, {}

    def project(rh):
        rows = jnp.concatenate([attended_of(rh * HL + h) for h in range(HL)], axis=1)

        def share(side, step):
            at = (side * 4 + (x + step) % 4) * COLS
            block = wo[:, pl.ds(pl.multiple_of(at, HD), COLS)]
            return jnp.dot(rows, block, preferred_element_type=F32)

        opp = [share(0, 2), share(1, 2)]
        for side in range(2):
            xopp[rh, side] = opp[side].astype(BF)
        xcopy[rh, "RR"] = send(
            xopp.at[rh, 0], xrel.at[rh, 0], xss.at[rh, 0], xrs.at[rh, 0], at_x(1)
        )
        xcopy[rh, "LL"] = send(
            xopp.at[rh, 1], xrel.at[rh, 1], xss.at[rh, 1], xrs.at[rh, 1], at_x(3)
        )
        sums = opp[0] + opp[1]
        r1 = share(1, 1)
        xs[rh, 0, 1] = r1.astype(BF)
        xcopy[rh, "R1"] = send(
            xs.at[rh, 0, 1], xfin.at[rh, 0, 1], xss.at[rh, 2], xrs.at[rh, 2], at_x(1)
        )
        l0 = share(0, 3)
        xs[rh, 1, 0] = l0.astype(BF)
        xcopy[rh, "L0"] = send(
            xs.at[rh, 1, 0], xfin.at[rh, 1, 0], xss.at[rh, 3], xrs.at[rh, 3], at_x(3)
        )
        r0 = share(0, 1)
        xf[rh, 2] = r0
        l1 = share(1, 3)
        xf[rh, 3] = l1
        sums = sums + r1 + l0 + r0 + l1
        for side in range(2):
            mine = share(side, 0)
            xf[rh, side] = mine
            sums = sums + mine
        turned = (sums[:, :HD] + sums[:, HD : 2 * HD] + sums[:, 2 * HD :]).T
        line = jnp.sum(turned, axis=0, keepdims=True) * D ** (-0.5)
        csb[rh, g] = jnp.broadcast_to(line, (8, BLK))
        for k in range(1, 8):
            ccopy[rh, k] = send(
                csb.at[rh, g], csb.at[rh, g], css.at[rh, k], crs.at[rh, k], (f, (g + k) % 8)
            )

    def relay_x(rh):
        xcopy[rh, "RR"].wait_recv()
        xs[rh, 0, 0] = (xf[rh, 2] + xrel[rh, 0].astype(F32)).astype(BF)
        xcopy[rh, "R0"] = send(
            xs.at[rh, 0, 0], xfin.at[rh, 0, 0], xss.at[rh, 4], xrs.at[rh, 4], at_x(1)
        )
        xcopy[rh, "LL"].wait_recv()
        xs[rh, 1, 1] = (xf[rh, 3] + xrel[rh, 1].astype(F32)).astype(BF)
        xcopy[rh, "L1"] = send(
            xs.at[rh, 1, 1], xfin.at[rh, 1, 1], xss.at[rh, 5], xrs.at[rh, 5], at_x(3)
        )

    def cross(rh):
        for name in ("R0", "R1", "L0", "L1"):
            xcopy[rh, name].wait_recv()
        other = 1 - zl
        zs[rh] = (
            xf[rh, other] + xfin[rh, 0, other].astype(F32) + xfin[rh, 1, other].astype(F32)
        ).astype(BF)
        xcopy[rh, "z"] = send(zs.at[rh], zr.at[rh], xss.at[rh, 6], xrs.at[rh, 6], zlo)

    def finish(rh):
        held = xf[rh, zl] + xfin[rh, 0, zl].astype(F32) + xfin[rh, 1, zl].astype(F32)
        xcopy[rh, "z"].wait_recv()
        out_ref[rh * BLK : (rh + 1) * BLK, :] = (held + zr[rh].astype(F32)).astype(BF)
        for k in range(1, 8):
            pltpu.make_async_remote_copy(
                src_ref=csb.at[rh, (g + 8 - k) % 8],
                dst_ref=csb.at[rh, (g + 8 - k) % 8],
                send_sem=css.at[rh, k],
                recv_sem=crs.at[rh, k],
                device_id=(f, (g + k) % 8),
                device_id_type=MESH,
            ).wait_recv()
        total = csb[rh, 0]
        for k in range(1, 8):
            total = total + csb[rh, k]
        cs_ref[rh] = total

    arrived_kv(0)
    arrived_q(0)
    attend(0)
    last_kv(2)
    arrived_kv(1)
    arrived_q(1)
    attend(1)
    relay_o(0)
    arrived_kv(2)
    arrived_q(2)
    attend(2)
    relay_o(1)
    attend(3)
    relay_o(2)
    attend(4)
    relay_o(3)
    wo_in.wait()
    project(0)
    attend(5)
    relay_o(4)
    relay_x(0)
    relay_o(5)
    cross(0)
    project(1)
    finish(0)
    relay_x(1)
    cross(1)
    finish(1)
    for copy in started:
        copy.wait_send()


def thresholds(near_mask, far_pattern, window, frame_id):
    blocks = jnp.arange(128, dtype=jnp.int32)
    slab = blocks // 2
    away = jnp.abs(slab - frame_id)
    limit = jnp.sum(
        jnp.where(
            jnp.arange(32, dtype=jnp.int32)[:, None] == away[None, :], window[:, None], 0
        ),
        axis=0,
    )
    far = jnp.pad(far_pattern, ((0, 0), (0, 64)))
    first = jnp.where(slab < frame_id, 0, 2)
    odd = blocks % 2
    near = jnp.where(
        first[None, :] == 0,
        jnp.where(odd[None, :] == 0, near_mask[:, 0:1], near_mask[:, 1:2]),
        jnp.where(odd[None, :] == 0, near_mask[:, 2:3], near_mask[:, 3:4]),
    )
    chosen = jnp.where(away[None, :] == 0, 1, jnp.where(away[None, :] == 1, near, far))
    table = jnp.where(chosen > 0, limit[None, :], 0).astype(F32)
    return jnp.pad(table, ((0, 6), (0, 0)))


def per_device(tokens, w_qkv, norm_gains, w_out, near_mask, far_pattern, window):
    table = thresholds(near_mask, far_pattern, window, lax.axis_index("frame"))
    any_spec = pl.BlockSpec(memory_space=pl.ANY)
    vmem_spec = pl.BlockSpec(memory_space=pltpu.VMEM)
    dma = pltpu.SemaphoreType.DMA
    out, checks = pl.pallas_call(
        layer_kernel,
        name="layer",
        out_shape=(
            jax.ShapeDtypeStruct((SLAB, COLS), BF),
            jax.ShapeDtypeStruct((2, 8, BLK), F32),
        ),
        in_specs=[any_spec, any_spec, any_spec, vmem_spec, vmem_spec],
        out_specs=(vmem_spec, vmem_spec),
        scratch_shapes=[
            pltpu.VMEM((SLAB, D), BF),
            pltpu.VMEM((HL, D, 2 * HD), BF),
            pltpu.VMEM((D, COLS), BF),
            pltpu.VMEM((COLS, D), BF),
            pltpu.VMEM((HL, 8, SLAB, 2 * HD), BF),
            pltpu.VMEM((HL, 4, SLAB, HD), BF),
            pltpu.VMEM((4, 8, 128), F32),
            pltpu.VMEM((8, 32, SLAB), F32),
            pltpu.VMEM((2, BLK, SLAB), F32),
            pltpu.VMEM((4 * BLK, 8 * SLAB), BF),
            pltpu.VMEM((6, BLK, HD), F32),
            pltpu.VMEM((6, BLK, HD), F32),
            pltpu.VMEM((6, 3, OROWS, HD), BF),
            pltpu.VMEM((6, CUT, HD), BF),
            pltpu.VMEM((6, OROWS - CUT, HD), BF),
            pltpu.VMEM((6, 2, OROWS, HD), BF),
            pltpu.VMEM((2, 4, BLK, COLS), F32),
            pltpu.VMEM((2, 2, BLK, COLS), BF),
            pltpu.VMEM((2, 2, BLK, COLS), BF),
            pltpu.VMEM((2, 2, 2, BLK, COLS), BF),
            pltpu.VMEM((2, 2, 2, BLK, COLS), BF),
            pltpu.VMEM((2, BLK, COLS), BF),
            pltpu.VMEM((2, BLK, COLS), BF),
            pltpu.VMEM((2, 8, 8, BLK), F32),
            dma((9,)),
            dma((HL, 8)),
            dma((HL, 8)),
            dma((HL, 4)),
            dma((HL, 4)),
            dma((3,)),
            dma((3,)),
            dma((6, 6)),
            dma((6, 6)),
            dma((2, 7)),
            dma((2, 7)),
            dma((2, 8)),
            dma((2, 8)),
        ],
        compiler_params=pltpu.CompilerParams(
            collective_id=0, has_side_effects=True, vmem_limit_bytes=56 * 1024 * 1024
        ),
    )(tokens, w_qkv, w_out, norm_gains, table)
    return out, checks[:, 0, :].reshape(SLAB)


def solution(mesh):
    in_specs = (
        P("frame", None),
        P(None, None, "head"),
        P(None, "head"),
        P("head", None),
        P("frame", None),
        P("frame", None),
        P(),
    )
    out_specs = (P("frame", "head"), P("frame"))
    return jax.shard_map(
        per_device, mesh=mesh, in_specs=in_specs, out_specs=out_specs, check_vma=False
    )
```

time: 267 us -> 76.2 us (0.29)
  waiting for transfers between devices: 146 us -> 0 us
  Pallas kernels: 0 us -> 69.2 us
  matrix products: 46.6 us -> 0 us
  local copies, waits for them, and re-layouts: 27.6 us -> 4.52 us
  blocking collectives: 19.8 us -> 0 us
  between operations: 14 us -> 0.65 us
  other arithmetic: 7.97 us -> 1.53 us
  starting transfers between devices: 4.64 us -> 0 us
    all_gather x2 -> x0, waiting for transfers between devices: 107 us -> none  [the longest x1 56 us: per_device(): lax.all_gather(values_flat, 'frame', axis=0, tiled=True)]
    pallas_call x0 -> x1, Pallas kernels: none -> 69.2 us  [per_device(): pl.pallas_call(layer_kernel, name='layer', out_shape=(jax.ShapeDtypeStruc...]
    dot_general x10 -> x0, matrix products: 46.6 us -> none  [the longest x2 18.1 us: attend(): jnp.einsum('qhd,khd->hqk', queries, key_heads, preferred_element_type=jnp...]
    unnamed x4 -> x0, waiting for transfers between devices: 39.1 us -> none
    psum x1 -> x0, blocking collectives: 19.8 us -> none  [per_device(): checksum = lax.psum(jnp.sum(full_rows, axis=1) * D ** (-0.5), 'head')]
    dot_general x3 -> x0, local copies, waits for them, and re-layouts: 13.7 us -> none  [the longest x2 9.4 us: per_device(): query = jnp.dot(tokens, w_qkv[0], preferred_element_type=jnp.float32)]
    all_gather x1 -> x0, local copies, waits for them, and re-layouts: 8.53 us -> none  [per_device(): lax.all_gather(values_flat, 'frame', axis=0, tiled=True)]
    and x3 -> x0, other arithmetic: 4.76 us -> none  [the longest x2 4.75 us: attend(): (chosen > 0.5) & inside[None, :]]
  transfers between devices with their start and end apart: 5 -> 0, of which waited for: 3 -> 0; matrix products, arithmetic and copies ran while one was open for 14% -> 0% of each run, Pallas kernels for 0% -> 0%
where the time goes in v1:
time: 76.2 us; the launch traced here: 75.9 us
  Pallas kernels  69.2 us (91%)
  local copies, waits for them, and re-layouts  4.52 us (6%)
  other arithmetic  1.53 us (2%)
    pallas_call x1, Pallas kernels, per_device(): pl.pallas_call(layer_kernel, name='layer', out_shape=(jax.ShapeDtypeStruc...  69.2 us
    unnamed x1, local copies, waits for them, and re-layouts  1.62 us

profile of v1, /device:TPU:2, one launch (start us, length us, event | category | flops | bytes accessed | tf_op | source)
XLA Modules:
  0.0 75.9 jit_solution(14030845471618792850)
XLA Ops:
  0.6 0.7 select_reduce_fusion
  1.4 1.0 %slice_reduce_fusion.3 = (s32[2]{0:T(128)S(1)}, s32[2]{0:T(128)S(1)}, s32[2]{0:T(128)S(1)}, s32[2]{0:T(128)S(1)}) fusion(s32[2,4]{1,0:T(2,128)} %param.11), kind=kLoop, calls=%fused_computation.10 | loop fusion | bytes 64 | tf_op jit(solution)/shard_map/slice | solution.py:425
  2.5 0.8 %fusion = f32[2,128]{1,0:T(2,128)S(1)} fusion(s32[2,64]{1,0:T(2,128)} %param.12, pred[128]{0:T(512)(128)(4,1)S(1)} %get-tuple-element.12, pred[128]{0:T(512)(128)(4,1)S(1)} %get-tuple-element.10, pred[128]{0:T(512)(128)(4,1)S(1)} %get-tuple-element.13, pred[128]{0:T(512)(128)(4,1)S(1)} %get-tuple-element.11, s32[128]{0:T(128)S(1)} %select_reduce_fusion, ...), kind=kLoop, calls=%fused_computation.6 | loop fusion | flops 2048 | bytes 2592 | tf_op jit(solution)/shard_map/convert_element_type | solution.py:429
  3.2 0.6 pad.9.thr_ref
  3.8 69.2 %layer.1 = (bf16[256,384]{1,0:T(8,128)(2,1)}, f32[2,8,128]{2,1,0:T(8,128)}) custom-call(bf16[256,3072]{1,0:T(8,128)(2,1)} %tok_hbm.1, bf16[3,3072,384]{2,1,0:T(8,128)(2,1)} %w_hbm.1, bf16[384,3072]{1,0:T(8,128)(2,1)} %wo_hbm.1, f32[2,384]{1,0:T(2,128)} %gains_ref.1, f32[8,128]{1,0:T(8,128)} %pad.9.thr_ref), custom_call_target="tpu_custom_call" | custom-call | tf_op jit(solution)/shard_map/layer/pallas_call | solution.py:438
  73.1 1.3 %slice.19 = f32[2,1,128]{2,1,0:T(1,128)} slice(f32[2,8,128]{2,1,0:T(8,128)} %get-tuple-element.5), slice={[0:2], [0:1], [0:128]} | slice | bytes 2048 | tf_op jit(solution)/shard_map/slice | solution.py:490
  74.3 1.6 %copy.10 = bf16[256,384]{1,0:T(8,128)(2,1)} copy(bf16[256,384]{1,0:T(8,128)(2,1)} %get-tuple-element.16) | data formatting | bytes 393216
  (3 shorter events, 0.0 us)

commit v2 on v0

v2 whole, which is shorter than its diff:
```python
import jax
import jax.numpy as jnp
from jax import lax
from jax.experimental import pallas as pl
from jax.experimental.pallas import tpu as pltpu
from jax.sharding import PartitionSpec as P

D = 3072
HD = 128
BLK = 128
SLAB = 256
HL = 3
COLS = HL * HD
POOL = 40
PART = 1024
MESH = pl.DeviceIdType.MESH
BF = jnp.bfloat16
F32 = jnp.float32
LOG2E = 1.4426950408889634
OROWS = BLK + 8
NT = (((1,), (1,)), ((), ()))


def layer_kernel(
    tok_hbm,
    w_hbm,
    wo_hbm,
    gains_hbm,
    near_hbm,
    far_hbm,
    window_hbm,
    out_ref,
    cs_ref,
    tok,
    wkv,
    wq,
    wx,
    kv,
    qb,
    gains_ref,
    near_ref,
    far_ref,
    window_ref,
    far,
    tbuf,
    texp,
    dist,
    pbuf,
    acc,
    num,
    tot,
    osend,
    orel,
    ofin,
    ab,
    po,
    zs,
    zr,
    csb,
    lsem,
    pool,
    krs,
    qrs,
    trs,
    wrs,
    ors,
    ars,
    zrs,
    crs,
):
    f = lax.axis_index("frame")
    g = lax.axis_index("head")
    zh, y, c = f // 8, (f // 2) % 4, f % 2
    zl, x = g // 4, g % 4

    def at_y(step):
        return (zh * 8 + ((y + step) % 4) * 2 + c, g)

    def at_z(step):
        return (((zh + step) % 4) * 8 + y * 2 + c, g)

    def at_x(step):
        return (f, zl * 4 + (x + step) % 4)

    core = (zh * 8 + y * 2 + (1 - c), g)
    zlo = (f, (1 - zl) * 4 + x)

    started = []
    waited = set()

    def sent(i):
        if i not in waited:
            waited.add(i)
            started[i].wait_send()

    def send(src, dst, rsem, dev):
        n = len(started)
        if n >= POOL:
            sent(n - POOL)
        copy = pltpu.make_async_remote_copy(
            src_ref=src,
            dst_ref=dst,
            send_sem=pool.at[n % POOL],
            recv_sem=rsem,
            device_id=dev,
            device_id_type=MESH,
        )
        copy.start()
        started.append(copy)
        return copy

    def fetch(src, dst, i):
        copy = pltpu.make_async_copy(src, dst, lsem.at[i])
        copy.start()
        return copy

    def columns(side, step):
        at = (side * 4 + (x + step) % 4) * COLS
        return pl.ds(pl.multiple_of(at, HD), COLS)

    barrier = pltpu.get_barrier_semaphore()
    peers = [at_y(1), at_y(3), core, at_z(1), at_z(3)]
    peers += [(f, (g + k) % 8) for k in range(1, 8)]
    for peer in peers:
        pl.semaphore_signal(barrier, inc=1, device_id=peer, device_id_type=MESH)

    small_in = [
        fetch(near_hbm, near_ref, 10),
        fetch(window_hbm, window_ref, 11),
        fetch(far_hbm, far_ref, 12),
        fetch(gains_hbm, gains_ref, 13),
    ]
    q_in = []
    for k in range(3):
        span = pl.ds(k * PART, PART)
        tok_at = fetch(tok_hbm.at[:, span], tok.at[:, span], (0, 14, 15)[k])
        q_in.append((tok_at, fetch(w_hbm.at[0, span], wq.at[span], (7, 16, 17)[k])))
    kv_in = []
    for h in range(HL):
        hs = pl.ds(h * HD, HD)
        kv_in.append(
            (
                fetch(w_hbm.at[1, :, hs], wkv.at[h, :, pl.ds(0, HD)], 1 + 2 * h),
                fetch(w_hbm.at[2, :, hs], wkv.at[h, :, pl.ds(HD, HD)], 2 + 2 * h),
            )
        )
    wx_in = (
        fetch(wo_hbm.at[:, columns(c, 0)], wx.at[0, 0], 8),
        fetch(wo_hbm.at[:, columns(1 - c, 0)], wx.at[0, 1], 9),
    )

    for copy in small_in:
        copy.wait()
    lane = lax.broadcasted_iota(jnp.int32, (8, 128), 1)
    line = lax.broadcasted_iota(jnp.int32, (8, 128), 0)
    slabs = lax.shift_right_logical(lane, 1)
    odd = lane - 2 * slabs
    apart = jnp.abs(slabs - f)
    limits = jnp.zeros((8, 128), jnp.int32)
    for d in range(32):
        limits = jnp.where(apart == d, window_ref[d], limits)
    near = []
    for a in range(2):
        before = jnp.where(odd == 1, near_ref[a, 1], near_ref[a, 0])
        after = jnp.where(odd == 1, near_ref[a, 3], near_ref[a, 2])
        near.append(jnp.where(slabs < f, before, after))
    far[...] = jnp.zeros((8, 128), jnp.int32)
    far[0:2, 0:64] = far_ref[...]
    chosen = jnp.where(apart == 1, jnp.where(line == 0, near[0], near[1]), far[...])
    chosen = jnp.where(apart == 0, 1, chosen)
    tbuf[0] = jnp.where(chosen > 0, limits, 0).astype(F32)

    def make_kv(h):
        for copy in kv_in[h]:
            copy.wait()
        both = jnp.dot(tok[...], wkv[h], preferred_element_type=F32)
        key = both[:, :HD]
        factor = lax.rsqrt(jnp.mean(key * key, axis=1, keepdims=True) + 1e-06)
        gain = gains_ref[1:2, h * HD : (h + 1) * HD]
        kv[h, 0, :, 0:HD] = (key * factor * gain).astype(BF)
        kv[h, 0, :, HD : 2 * HD] = both[:, HD:].astype(BF)

    def make_q():
        whole = None
        for k in range(3):
            for copy in q_in[k]:
                copy.wait()
            span = slice(k * PART, (k + 1) * PART)
            part = jnp.dot(tok[:, span], wq[span, :], preferred_element_type=F32)
            whole = part if whole is None else whole + part
        for h in range(HL):
            query = whole[:, h * HD : (h + 1) * HD]
            factor = lax.rsqrt(jnp.mean(query * query, axis=1, keepdims=True) + 1e-06)
            gain = gains_ref[0:1, h * HD : (h + 1) * HD] * (HD**-0.5 * LOG2E)
            qb[h, 0] = (query * factor * gain).astype(BF)

    top, low = pl.ds(0, BLK), pl.ds(BLK, BLK)
    kcopy, qcopy, tcopy, wcopy, ocopy, acopy = {}, {}, {}, {}, {}, {}

    def send_kv(h):
        own = kv.at[h, 0]
        kcopy[h, "R"] = send(own, kv.at[h, 1], krs.at[h, 0], at_y(1))
        kcopy[h, "L"] = send(own, kv.at[h, 2], krs.at[h, 1], at_y(3))
        kcopy[h, "c0"] = send(own, kv.at[h, 4], krs.at[h, 2], core)

    def relay_kv(h):
        kcopy[h, "R"].wait_recv()
        kcopy[h, "RR"] = send(
            kv.at[h, 1, top], kv.at[h, 3, top], krs.at[h, 3], at_y(1)
        )
        kcopy[h, "c1"] = send(kv.at[h, 1], kv.at[h, 5], krs.at[h, 4], core)
        kcopy[h, "L"].wait_recv()
        kcopy[h, "LL"] = send(
            kv.at[h, 2, low], kv.at[h, 3, low], krs.at[h, 5], at_y(3)
        )
        kcopy[h, "c2"] = send(kv.at[h, 2], kv.at[h, 6], krs.at[h, 6], core)

    def last_kv(h):
        kcopy[h, "RR"].wait_recv()
        kcopy[h, "LL"].wait_recv()
        kcopy[h, "c3"] = send(kv.at[h, 3], kv.at[h, 7], krs.at[h, 7], core)

    def arrived_kv(h):
        for name in ("c0", "c1", "c2", "c3"):
            kcopy[h, name].wait_recv()

    def send_ring(buf, copies, rsem, to, h):
        own = buf.at[h, 0]
        copies[h, "R"] = send(own, buf.at[h, 1], rsem.at[h, 0], to(1))
        copies[h, "L"] = send(own, buf.at[h, 2], rsem.at[h, 1], to(3))

    def relay_ring(buf, copies, rsem, to, h):
        copies[h, "R"].wait_recv()
        copies[h, "RR"] = send(
            buf.at[h, 1, top], buf.at[h, 3, top], rsem.at[h, 2], to(1)
        )
        copies[h, "L"].wait_recv()
        copies[h, "LL"] = send(
            buf.at[h, 2, low], buf.at[h, 3, low], rsem.at[h, 3], to(3)
        )

    def arrived_ring(copies, h):
        copies[h, "RR"].wait_recv()
        copies[h, "LL"].wait_recv()

    def send_q(h):
        send_ring(qb, qcopy, qrs, at_z, h)

    def relay_q(h):
        relay_ring(qb, qcopy, qrs, at_z, h)

    def arrived_q(h):
        arrived_ring(qcopy, h)

    def send_t():
        tcopy["R"] = send(tbuf.at[0], tbuf.at[1], trs.at[0], at_z(1))
        tcopy["L"] = send(tbuf.at[0], tbuf.at[2], trs.at[1], at_z(3))

    def relay_t():
        tcopy["R"].wait_recv()
        tcopy["RR"] = send(tbuf.at[1], tbuf.at[3], trs.at[2], at_z(1))
        tcopy["L"].wait_recv()

    def send_w():
        for k, step in ((1, 1), (2, 3), (3, 2)):
            wcopy[k] = send(
                wo_hbm.at[:, columns(c, step)], wx.at[k, 0], wrs.at[k], at_x(step)
            )

    def share_w():
        for k in (1, 2, 3):
            wcopy[k].wait_recv()
            wcopy[k + 3] = send(wx.at[k, 0], wx.at[k, 1], wrs.at[k + 3], core)

    def arrived_w():
        for copy in wx_in:
            copy.wait()
        for k in (4, 5, 6):
            wcopy[k].wait_recv()

    def limits_table():
        row = lax.broadcasted_iota(jnp.int32, (BLK, SLAB), 0)
        col = lax.broadcasted_iota(jnp.int32, (BLK, SLAB), 1)
        for rh in range(2):
            dist[rh] = jnp.abs(row + rh * BLK - col).astype(F32)
        tcopy["RR"].wait_recv()
        table = tbuf[...].reshape(4 * 8, 128).astype(BF)
        half = (col >= BLK).astype(jnp.int32)
        for j in range(8):
            slab = zh * 8 + ((y + (0, 3, 1, 2)[j % 4]) % 4) * 2 + (c if j < 4 else 1 - c)
            pick = (row == half + slab * 2).astype(F32).astype(BF)
            texp[j] = jnp.dot(table, pick, preferred_element_type=F32)

    def attend(h, slots):
        size = SLAB * len(slots)
        queries = jnp.concatenate([qb[h, q] for q in slots], axis=0)

        for k in range(4):
            pair = slice(2 * k, 2 * k + 2)
            cols = slice(2 * k * SLAB, (2 * k + 2) * SLAB)
            for j in range(2 * k, 2 * k + 2):
                raw = lax.dot_general(queries, kv[h, j, :, 0:HD], NT, preferred_element_type=F32)
                for i, q in enumerate(slots):
                    for rh in range(2):
                        rows = slice(i * SLAB + rh * BLK, i * SLAB + (rh + 1) * BLK)
                        limit = texp[j, q * 8 + rh : q * 8 + rh + 1, :]
                        weight = jnp.where(dist[rh] < limit, jnp.exp2(raw[rows]), 0.0)
                        pbuf[rows, j * SLAB : (j + 1) * SLAB] = weight.astype(BF)
            values = kv[h, pair, :, HD : 2 * HD].reshape(2 * SLAB, HD)
            values = jnp.concatenate([values, jnp.ones((2 * SLAB, HD), BF)], axis=1)
            part = jnp.dot(pbuf[0:size, cols], values, preferred_element_type=F32)
            if k == 0:
                acc[0:size, :] = part
            else:
                acc[0:size, :] += part
        return acc[0:size, :]

    def pack(h, dest, part):
        for half in range(2):
            rows = part[half * BLK : (half + 1) * BLK]
            osend[h, dest, half, 0:BLK, :] = rows[:, :HD].astype(BF)
            osend[h, dest, half, BLK:OROWS, :] = rows[:, HD:].T[0:8].astype(BF)

    def attend_opp(h):
        pack(h, 2, attend(h, (3,)))
        ocopy[h, "RR"] = send(
            osend.at[h, 2, 0], orel.at[h, 0], ors.at[h, 0], at_z(1)
        )
        ocopy[h, "LL"] = send(
            osend.at[h, 2, 1], orel.at[h, 1], ors.at[h, 1], at_z(3)
        )

    def attend_sides(h):
        result = attend(h, (1, 2))
        pack(h, 0, result[:SLAB])
        pack(h, 1, result[SLAB:])
        ocopy[h, "R1"] = send(
            osend.at[h, 1, 1], ofin.at[h, 0, 1], ors.at[h, 2], at_z(1)
        )
        ocopy[h, "L0"] = send(
            osend.at[h, 0, 0], ofin.at[h, 1, 0], ors.at[h, 3], at_z(3)
        )

    def relay_o(h):
        ocopy[h, "RR"].wait_recv()
        osend[h, 1, 0] = (osend[h, 1, 0].astype(F32) + orel[h, 0].astype(F32)).astype(BF)
        ocopy[h, "R0"] = send(
            osend.at[h, 1, 0], ofin.at[h, 0, 0], ors.at[h, 4], at_z(1)
        )
        ocopy[h, "LL"].wait_recv()
        osend[h, 0, 1] = (osend[h, 0, 1].astype(F32) + orel[h, 1].astype(F32)).astype(BF)
        ocopy[h, "L1"] = send(
            osend.at[h, 0, 1], ofin.at[h, 1, 1], ors.at[h, 5], at_z(3)
        )

    def attend_own(h):
        result = attend(h, (0,))
        num[h] = result[:, :HD]
        tot[h] = result[:, HD:]

    def combine(h):
        for name in ("R0", "R1", "L0", "L1"):
            ocopy[h, name].wait_recv()
        for half in range(2):
            more = ofin[h, 0, half].astype(F32) + ofin[h, 1, half].astype(F32)
            rows = slice(half * BLK, (half + 1) * BLK)
            strip = more[BLK:OROWS]
            total = tot[h, rows, :] + jnp.concatenate([strip] * 16, axis=0).T
            ab[h, 0, rows, :] = ((num[h, rows, :] + more[:BLK]) / total).astype(BF)
        send_ring(ab, acopy, ars, at_x, h)

    def relay_a(h):
        relay_ring(ab, acopy, ars, at_x, h)

    def arrived_a(h):
        arrived_ring(acopy, h)

    def last_rows(pair, side):
        rows = jnp.concatenate([ab[2, pair], ab[2, pair + 1]], axis=1)
        block = jnp.concatenate(
            [wx[pair, side, 2 * HD : COLS, :], wx[pair + 1, side, 2 * HD : COLS, :]], axis=0
        )
        return jnp.dot(rows, block, preferred_element_type=F32)

    def project_first():
        for side in range(2):
            total = None
            for k in range(4):
                rows = jnp.concatenate([ab[0, k], ab[1, k]], axis=1)
                part = jnp.dot(rows, wx[k, side, 0 : 2 * HD, :], preferred_element_type=F32)
                total = part if total is None else total + part
            po[side] = total

    def project_near():
        for side in range(2):
            po[side] = po[side] + last_rows(0, side)

    def finish():
        other = (c + zl + 1) % 2
        given = po[other] + last_rows(2, other)
        zs[...] = given.astype(BF)
        zcopy = send(zs, zr, zrs.at[0], zlo)
        kept = po[1 - other] + last_rows(2, 1 - other)
        sums = given + kept
        turned = (sums[:, :HD] + sums[:, HD : 2 * HD] + sums[:, 2 * HD :]).T
        total = jnp.sum(turned, axis=0, keepdims=True) * D ** (-0.5)
        csb[g] = jnp.broadcast_to(total, (8, SLAB))
        for k in range(1, 8):
            send(csb.at[g], csb.at[g], crs.at[k], (f, (g + k) % 8))
        po[0] = kept
        for k in range(1, 8):
            pltpu.make_async_remote_copy(
                src_ref=csb.at[(g + 8 - k) % 8],
                dst_ref=csb.at[(g + 8 - k) % 8],
                send_sem=pool.at[0],
                recv_sem=crs.at[k],
                device_id=(f, (g + k) % 8),
                device_id_type=MESH,
            ).wait_recv()
        checks = csb[0]
        for k in range(1, 8):
            checks = checks + csb[k]
        cs_ref[...] = checks[0]
        zcopy.wait_recv()
        out_ref[...] = (po[0] + zr[...].astype(F32)).astype(BF)

    def drain():
        for i in range(len(started)):
            sent(i)

    make_q()
    pl.semaphore_wait(barrier, len(peers))
    send_t()
    send_q(0)
    send_q(1)
    send_q(2)
    make_kv(0)
    send_kv(0)
    make_kv(1)
    send_kv(1)
    make_kv(2)
    send_kv(2)
    send_w()
    relay_t()
    relay_q(0)
    relay_kv(0)
    relay_q(1)
    relay_kv(1)
    relay_q(2)
    relay_kv(2)
    last_kv(0)
    limits_table()
    arrived_q(0)
    arrived_kv(0)
    attend_opp(0)
    last_kv(1)
    attend_sides(0)
    last_kv(2)
    arrived_kv(1)
    arrived_q(1)
    attend_opp(1)
    arrived_kv(2)
    arrived_q(2)
    attend_opp(2)
    attend_sides(1)
    relay_o(0)
    attend_sides(2)
    share_w()
    attend_own(0)
    relay_o(1)
    attend_own(1)
    attend_own(2)
    relay_o(2)
    combine(0)
    combine(1)
    arrived_w()
    relay_a(0)
    combine(2)
    relay_a(1)
    drain()
    relay_a(2)
    arrived_a(0)
    arrived_a(1)
    project_first()
    project_near()
    arrived_a(2)
    finish()
    drain()


def per_device(tokens, w_qkv, norm_gains, w_out, near_mask, far_pattern, window):
    any_spec = pl.BlockSpec(memory_space=pl.ANY)
    vmem_spec = pl.BlockSpec(memory_space=pltpu.VMEM)
    dma = pltpu.SemaphoreType.DMA
    return pl.pallas_call(
        layer_kernel,
        name="layer",
        out_shape=(
            pltpu.VMEM((SLAB, COLS), BF),
            pltpu.VMEM((SLAB,), F32),
        ),
        in_specs=[any_spec] * 7,
        out_specs=(vmem_spec, vmem_spec),
        scratch_shapes=[
            pltpu.VMEM((SLAB, D), BF),
            pltpu.VMEM((HL, D, 2 * HD), BF),
            pltpu.VMEM((D, COLS), BF),
            pltpu.VMEM((4, 2, COLS, COLS), BF),
            pltpu.VMEM((HL, 8, SLAB, 2 * HD), BF),
            pltpu.VMEM((HL, 4, SLAB, HD), BF),
            pltpu.VMEM((2, COLS), F32),
            pltpu.SMEM((2, 4), jnp.int32),
            pltpu.VMEM((2, 64), jnp.int32),
            pltpu.SMEM((32,), jnp.int32),
            pltpu.VMEM((8, 128), jnp.int32),
            pltpu.VMEM((4, 8, 128), F32),
            pltpu.VMEM((8, 32, SLAB), F32),
            pltpu.VMEM((2, BLK, SLAB), F32),
            pltpu.VMEM((2 * SLAB, 8 * SLAB), BF),
            pltpu.VMEM((2 * SLAB, 2 * HD), F32),
            pltpu.VMEM((HL, SLAB, HD), F32),
            pltpu.VMEM((HL, SLAB, HD), F32),
            pltpu.VMEM((HL, 3, 2, OROWS, HD), BF),
            pltpu.VMEM((HL, 2, OROWS, HD), BF),
            pltpu.VMEM((HL, 2, 2, OROWS, HD), BF),
            pltpu.VMEM((HL, 4, SLAB, HD), BF),
            pltpu.VMEM((2, SLAB, COLS), F32),
            pltpu.VMEM((SLAB, COLS), BF),
            pltpu.VMEM((SLAB, COLS), BF),
            pltpu.VMEM((8, 8, SLAB), F32),
            dma((14 + 4,)),
            dma((POOL,)),
            dma((HL, 8)),
            dma((HL, 4)),
            dma((3,)),
            dma((7,)),
            dma((HL, 6)),
            dma((HL, 4)),
            dma((1,)),
            dma((8,)),
        ],
        compiler_params=pltpu.CompilerParams(
            collective_id=0, has_side_effects=True, vmem_limit_bytes=56 * 1024 * 1024
        ),
    )(tokens, w_qkv, w_out, norm_gains, near_mask, far_pattern, window)


def solution(mesh):
    in_specs = (
        P("frame", None),
        P(None, None, "head"),
        P(None, "head"),
        P("head", None),
        P("frame", None),
        P("frame", None),
        P(),
    )
    out_specs = (P("frame", "head"), P("frame"))
    return jax.shard_map(
        per_device, mesh=mesh, in_specs=in_specs, out_specs=out_specs, check_vma=False
    )
```

time: 267 us -> 60.4 us (0.23)
  waiting for transfers between devices: 146 us -> 0 us
  Pallas kernels: 0 us -> 58 us
  matrix products: 46.6 us -> 0 us
  local copies, waits for them, and re-layouts: 27.6 us -> 1.24 us
  blocking collectives: 19.8 us -> 0 us
  between operations: 14 us -> 0.64 us
  other arithmetic: 7.97 us -> 0 us
  starting transfers between devices: 4.64 us -> 0 us
    all_gather x2 -> x0, waiting for transfers between devices: 107 us -> none  [the longest x1 56 us: per_device(): lax.all_gather(values_flat, 'frame', axis=0, tiled=True)]
    pallas_call x0 -> x1, Pallas kernels: none -> 58 us  [per_device(): pl.pallas_call(layer_kernel, name='layer', out_shape=(pltpu.VMEM((SLAB, C...]
    dot_general x10 -> x0, matrix products: 46.6 us -> none  [the longest x2 18.1 us: attend(): jnp.einsum('qhd,khd->hqk', queries, key_heads, preferred_element_type=jnp...]
    unnamed x4 -> x0, waiting for transfers between devices: 39.1 us -> none
    psum x1 -> x0, blocking collectives: 19.8 us -> none  [per_device(): checksum = lax.psum(jnp.sum(full_rows, axis=1) * D ** (-0.5), 'head')]
    dot_general x3 -> x0, local copies, waits for them, and re-layouts: 13.7 us -> none  [the longest x2 9.4 us: per_device(): query = jnp.dot(tokens, w_qkv[0], preferred_element_type=jnp.float32)]
    all_gather x1 -> x0, local copies, waits for them, and re-layouts: 8.53 us -> none  [per_device(): lax.all_gather(values_flat, 'frame', axis=0, tiled=True)]
    and x3 -> x0, other arithmetic: 4.76 us -> none  [the longest x2 4.75 us: attend(): (chosen > 0.5) & inside[None, :]]
  transfers between devices with their start and end apart: 5 -> 0, of which waited for: 3 -> 0; matrix products, arithmetic and copies ran while one was open for 14% -> 0% of each run, Pallas kernels for 0% -> 0%
where the time goes in v2:
time: 60.4 us; the launch traced here: 59.9 us
  Pallas kernels  58 us (96%)
  local copies, waits for them, and re-layouts  1.24 us (2%)
  between operations  0.64 us (1%)
    pallas_call x1, Pallas kernels, per_device(): pl.pallas_call(layer_kernel, name='layer', out_shape=(pltpu.VMEM((SLAB, C...  58 us
    unnamed x2, local copies, waits for them, and re-layouts  1.24 us

profile of v2, /device:TPU:2, one launch (start us, length us, event | category | flops | bytes accessed | tf_op | source)
XLA Modules:
  0.0 59.9 jit_solution(5995096562990189619)
XLA Ops:
  0.6 58.0 %layer.1 = (bf16[256,384]{1,0:T(8,128)(2,1)S(1)}, f32[256]{0:T(256)S(1)}) custom-call(bf16[256,3072]{1,0:T(8,128)(2,1)} %tok_hbm.1, bf16[3,3072,384]{2,1,0:T(8,128)(2,1)} %w_hbm.1, bf16[384,3072]{1,0:T(8,128)(2,1)} %wo_hbm.1, f32[2,384]{1,0:T(2,128)} %gains_hbm.1, s32[2,4]{1,0:T(2,128)} %near_hbm.1, s32[2,64]{1,0:T(2,128)} %far_hbm.1, s32[32]{0:T(128)} %window_hbm.1), custom_call_target="tpu_custom_call" | custom-call | tf_op jit(solution)/shard_map/layer/pallas_call | solution.py:495
  58.6 0.7 %copy.11 = bf16[256,384]{1,0:T(8,128)(2,1)} copy(bf16[256,384]{1,0:T(8,128)(2,1)S(1)} %get-tuple-element.2) | data formatting | bytes 393216
  59.3 0.6 copy.12

commit v3 on v2

--- a/solution.py
+++ b/solution.py
@@ -57,7 +57,6 @@
     zs,
     zr,
     csb,
-    lsem,
     pool,
     krs,
     qrs,
@@ -110,7 +109,7 @@
         return copy
 
     def fetch(src, dst, i):
-        copy = pltpu.make_async_copy(src, dst, lsem.at[i])
+        copy = pltpu.make_async_copy(src, dst, pool.at[POOL - 21 + i])
         copy.start()
         return copy
 
@@ -130,23 +129,29 @@
         fetch(far_hbm, far_ref, 12),
         fetch(gains_hbm, gains_ref, 13),
     ]
-    q_in = []
+    kv_in = []
     for k in range(3):
         span = pl.ds(k * PART, PART)
-        tok_at = fetch(tok_hbm.at[:, span], tok.at[:, span], (0, 14, 15)[k])
-        q_in.append((tok_at, fetch(w_hbm.at[0, span], wq.at[span], (7, 16, 17)[k])))
-    kv_in = []
-    for h in range(HL):
-        hs = pl.ds(h * HD, HD)
         kv_in.append(
             (
-                fetch(w_hbm.at[1, :, hs], wkv.at[h, :, pl.ds(0, HD)], 1 + 2 * h),
-                fetch(w_hbm.at[2, :, hs], wkv.at[h, :, pl.ds(HD, HD)], 2 + 2 * h),
+                fetch(tok_hbm.at[:, span], tok.at[:, span], 3 * k),
+                fetch(w_hbm.at[1, span, pl.ds(0, HD)], wkv.at[0, span, pl.ds(0, HD)], 3 * k + 1),
+                fetch(w_hbm.at[2, span, pl.ds(0, HD)], wkv.at[0, span, pl.ds(HD, HD)], 3 * k + 2),
             )
         )
+    first, rest = pl.ds(0, HD), pl.ds(HD, 2 * HD)
+    q_first = fetch(w_hbm.at[0, :, first], wq.at[:, first], 14)
+    q_rest = fetch(w_hbm.at[0, :, rest], wq.at[:, rest], 15)
+    later_in = {}
+    for h in (1, 2):
+        hs = pl.ds(h * HD, HD)
+        later_in[h] = (
+            fetch(w_hbm.at[1, :, hs], wkv.at[h, :, pl.ds(0, HD)], 14 + 2 * h),
+            fetch(w_hbm.at[2, :, hs], wkv.at[h, :, pl.ds(HD, HD)], 15 + 2 * h),
+        )
     wx_in = (
-        fetch(wo_hbm.at[:, columns(c, 0)], wx.at[0, 0], 8),
-        fetch(wo_hbm.at[:, columns(1 - c, 0)], wx.at[0, 1], 9),
+        fetch(wo_hbm.at[:, columns(c, 0)], wx.at[0, 0], 9),
+        fetch(wo_hbm.at[:, columns(1 - c, 0)], wx.at[0, 1], 20),
     )
 
     for copy in small_in:
@@ -170,29 +175,42 @@
     chosen = jnp.where(apart == 0, 1, chosen)
     tbuf[0] = jnp.where(chosen > 0, limits, 0).astype(F32)
 
-    def make_kv(h):
-        for copy in kv_in[h]:
-            copy.wait()
-        both = jnp.dot(tok[...], wkv[h], preferred_element_type=F32)
+    def keep_kv(h, both):
         key = both[:, :HD]
         factor = lax.rsqrt(jnp.mean(key * key, axis=1, keepdims=True) + 1e-06)
         gain = gains_ref[1:2, h * HD : (h + 1) * HD]
         kv[h, 0, :, 0:HD] = (key * factor * gain).astype(BF)
         kv[h, 0, :, HD : 2 * HD] = both[:, HD:].astype(BF)
 
-    def make_q():
-        whole = None
+    def make_first():
+        both = None
         for k in range(3):
-            for copy in q_in[k]:
+            for copy in kv_in[k]:
                 copy.wait()
             span = slice(k * PART, (k + 1) * PART)
-            part = jnp.dot(tok[:, span], wq[span, :], preferred_element_type=F32)
-            whole = part if whole is None else whole + part
-        for h in range(HL):
-            query = whole[:, h * HD : (h + 1) * HD]
-            factor = lax.rsqrt(jnp.mean(query * query, axis=1, keepdims=True) + 1e-06)
-            gain = gains_ref[0:1, h * HD : (h + 1) * HD] * (HD**-0.5 * LOG2E)
-            qb[h, 0] = (query * factor * gain).astype(BF)
+            part = jnp.dot(tok[:, span], wkv[0, span, :], preferred_element_type=F32)
+            both = part if both is None else both + part
+        keep_kv(0, both)
+
+    def make_kv(h):
+        for copy in later_in[h]:
+            copy.wait()
+        keep_kv(h, jnp.dot(tok[...], wkv[h], preferred_element_type=F32))
+
+    def keep_q(h, query):
+        factor = lax.rsqrt(jnp.mean(query * query, axis=1, keepdims=True) + 1e-06)
+        gain = gains_ref[0:1, h * HD : (h + 1) * HD] * (HD**-0.5 * LOG2E)
+        qb[h, 0] = (query * factor * gain).astype(BF)
+
+    def make_q():
+        q_first.wait()
+        keep_q(0, jnp.dot(tok[...], wq[:, 0:HD], preferred_element_type=F32))
+
+    def make_rest():
+        q_rest.wait()
+        both = jnp.dot(tok[...], wq[:, HD:], preferred_element_type=F32)
+        keep_q(1, both[:, :HD])
+        keep_q(2, both[:, HD:])
 
     top, low = pl.ds(0, BLK), pl.ds(BLK, BLK)
     kcopy, qcopy, tcopy, wcopy, ocopy, acopy = {}, {}, {}, {}, {}, {}
@@ -273,8 +291,6 @@
             wcopy[k + 3] = send(wx.at[k, 0], wx.at[k, 1], wrs.at[k + 3], core)
 
     def arrived_w():
-        for copy in wx_in:
-            copy.wait()
         for k in (4, 5, 6):
             wcopy[k].wait_recv()
 
@@ -424,60 +440,64 @@
         zcopy.wait_recv()
         out_ref[...] = (po[0] + zr[...].astype(F32)).astype(BF)
 
-    def drain():
-        for i in range(len(started)):
+    def drain(count):
+        for i in range(count):
             sent(i)
 
-    make_q()
+    make_first()
     pl.semaphore_wait(barrier, len(peers))
     send_t()
+    send_kv(0)
+    make_q()
     send_q(0)
+    make_rest()
     send_q(1)
-    send_q(2)
-    make_kv(0)
-    send_kv(0)
     make_kv(1)
     send_kv(1)
+    for copy in wx_in:
+        copy.wait()
     make_kv(2)
-    send_kv(2)
     send_w()
     relay_t()
+    relay_kv(0)
+    send_kv(2)
     relay_q(0)
-    relay_kv(0)
+    send_q(2)
+    relay_kv(1)
+    last_kv(0)
     relay_q(1)
-    relay_kv(1)
-    relay_q(2)
+    limits_table()
+    arrived_kv(0)
+    attend_sides(0)
     relay_kv(2)
-    last_kv(0)
-    limits_table()
     arrived_q(0)
-    arrived_kv(0)
     attend_opp(0)
     last_kv(1)
-    attend_sides(0)
+    relay_q(2)
+    early = len(started)
+    arrived_kv(1)
+    attend_sides(1)
     last_kv(2)
-    arrived_kv(1)
     arrived_q(1)
     attend_opp(1)
     arrived_kv(2)
     arrived_q(2)
     attend_opp(2)
-    attend_sides(1)
+    attend_sides(2)
     relay_o(0)
-    attend_sides(2)
     share_w()
     attend_own(0)
     relay_o(1)
     attend_own(1)
     attend_own(2)
     relay_o(2)
+    drain(early)
+    arrived_w()
     combine(0)
     combine(1)
-    arrived_w()
     relay_a(0)
     combine(2)
     relay_a(1)
-    drain()
     relay_a(2)
     arrived_a(0)
     arrived_a(1)
@@ -485,14 +505,25 @@
     project_near()
     arrived_a(2)
     finish()
-    drain()
+    drain(len(started))
+
+
+def place_kernel(rows_ref, sums_ref, rows_hbm, sums_hbm, sem):
+    copies = [
+        pltpu.make_async_copy(rows_ref, rows_hbm, sem.at[0]),
+        pltpu.make_async_copy(sums_ref, sums_hbm, sem.at[1]),
+    ]
+    for copy in copies:
+        copy.start()
+    for copy in copies:
+        copy.wait()
 
 
 def per_device(tokens, w_qkv, norm_gains, w_out, near_mask, far_pattern, window):
     any_spec = pl.BlockSpec(memory_space=pl.ANY)
     vmem_spec = pl.BlockSpec(memory_space=pltpu.VMEM)
     dma = pltpu.SemaphoreType.DMA
-    return pl.pallas_call(
+    held = pl.pallas_call(
         layer_kernel,
         name="layer",
         out_shape=(
@@ -528,7 +559,6 @@
             pltpu.VMEM((SLAB, COLS), BF),
             pltpu.VMEM((SLAB, COLS), BF),
             pltpu.VMEM((8, 8, SLAB), F32),
-            dma((14 + 4,)),
             dma((POOL,)),
             dma((HL, 8)),
             dma((HL, 4)),
@@ -543,6 +573,17 @@
             collective_id=0, has_side_effects=True, vmem_limit_bytes=56 * 1024 * 1024
         ),
     )(tokens, w_qkv, w_out, norm_gains, near_mask, far_pattern, window)
+    return pl.pallas_call(
+        place_kernel,
+        name="place",
+        out_shape=(
+            jax.ShapeDtypeStruct((SLAB, COLS), BF),
+            jax.ShapeDtypeStruct((SLAB,), F32),
+        ),
+        in_specs=[vmem_spec, vmem_spec],
+        out_specs=(any_spec, any_spec),
+        scratch_shapes=[dma((2,))],
+    )(*(pltpu.with_memory_space_constraint(part, pltpu.VMEM) for part in held))
 
 
 def solution(mesh):

time: 60.4 us -> 60.3 us (level)
  Pallas kernels: 58 us -> 59.5 us
  local copies, waits for them, and re-layouts: 1.24 us -> 0 us
    unnamed x2 -> x0, local copies, waits for them, and re-layouts: 1.24 us -> none
    pallas_call x1, Pallas kernels: 58 us -> 58.8 us  [per_device(): pl.pallas_call(layer_kernel, name='layer', out_shape=(pltpu.VMEM((SLAB, C...]
    pallas_call x0 -> x1, Pallas kernels: none -> 0.7 us  [per_device(): pl.pallas_call(place_kernel, name='place', out_shape=(jax.ShapeDtypeStruc...]
where the time goes in v3:
time: 60.3 us; the launch traced here: 60.2 us
  Pallas kernels  59.5 us (99%)
  between operations  0.64 us (1%)
    pallas_call x1, Pallas kernels, per_device(): pl.pallas_call(layer_kernel, name='layer', out_shape=(pltpu.VMEM((SLAB, C...  58.8 us

profile of v3, /device:TPU:2, one launch (start us, length us, event | category | flops | bytes accessed | tf_op | source)
XLA Modules:
  0.0 60.2 jit_solution(8491182159250104919)
XLA Ops:
  0.6 58.8 %layer.1 = (bf16[256,384]{1,0:T(8,128)(2,1)S(1)}, f32[256]{0:T(256)S(1)}) custom-call(bf16[256,3072]{1,0:T(8,128)(2,1)} %tok_hbm.1, bf16[3,3072,384]{2,1,0:T(8,128)(2,1)} %w_hbm.1, bf16[384,3072]{1,0:T(8,128)(2,1)} %wo_hbm.1, f32[2,384]{1,0:T(2,128)} %gains_hbm.1, s32[2,4]{1,0:T(2,128)} %near_hbm.1, s32[2,64]{1,0:T(2,128)} %far_hbm.1, s32[32]{0:T(128)} %window_hbm.1), custom_call_target="tpu_custom_call" | custom-call | tf_op jit(solution)/shard_map/layer/pallas_call | solution.py:526
  59.5 0.7 %place.1 = (bf16[256,384]{1,0:T(8,128)(2,1)}, f32[256]{0:T(256)}) custom-call(bf16[256,384]{1,0:T(8,128)(2,1)S(1)} %get-tuple-element.4.rows_ref, f32[256]{0:T(256)S(1)} %get-tuple-element.5.sums_ref), custom_call_target="tpu_custom_call" | custom-call | tf_op jit(solution)/shard_map/place/pallas_call | solution.py:576

commit v4 on v3

--- a/solution.py
+++ b/solution.py
@@ -35,6 +35,9 @@
     wkv,
     wq,
     wx,
+    wo,
+    rs,
+    csp,
     kv,
     qb,
     gains_ref,
@@ -109,7 +112,7 @@
         return copy
 
     def fetch(src, dst, i):
-        copy = pltpu.make_async_copy(src, dst, pool.at[POOL - 21 + i])
+        copy = pltpu.make_async_copy(src, dst, pool.at[POOL - 22 + i])
         copy.start()
         return copy
 
@@ -152,6 +155,7 @@
     wx_in = (
         fetch(wo_hbm.at[:, columns(c, 0)], wx.at[0, 0], 9),
         fetch(wo_hbm.at[:, columns(1 - c, 0)], wx.at[0, 1], 20),
+        fetch(wo_hbm, wo, 21),
     )
 
     for copy in small_in:
@@ -307,6 +311,12 @@
             pick = (row == half + slab * 2).astype(F32).astype(BF)
             texp[j] = jnp.dot(table, pick, preferred_element_type=F32)
 
+    def row_sums():
+        whole = jnp.dot(wo[...], jnp.ones((D, HD), BF), preferred_element_type=F32)
+        high = whole.astype(BF)
+        rs[:, 0:HD] = high
+        rs[:, HD:] = (whole - high.astype(F32)).astype(BF)
+
     def attend(h, slots):
         size = SLAB * len(slots)
         queries = jnp.concatenate([qb[h, q] for q in slots], axis=0)
@@ -383,7 +393,29 @@
             strip = more[BLK:OROWS]
             total = tot[h, rows, :] + jnp.concatenate([strip] * 16, axis=0).T
             ab[h, 0, rows, :] = ((num[h, rows, :] + more[:BLK]) / total).astype(BF)
-        send_ring(ab, acopy, ars, at_x, h)
+            if h == 2:
+                part = (top, low)[half]
+                own = ab.at[h, 0, part]
+                acopy[h, "R", half] = send(own, ab.at[h, 1, part], ars.at[h, half], at_x(1))
+                acopy[h, "L", half] = send(own, ab.at[h, 2, part], ars.at[h, 2 + half], at_x(3))
+        if h < 2:
+            send_ring(ab, acopy, ars, at_x, h)
+        both = jnp.dot(ab[h, 0], rs[h * HD : (h + 1) * HD, :], preferred_element_type=F32)
+        if h == 0:
+            csp[...] = both[:, :HD] + both[:, HD:]
+        else:
+            csp[...] += both[:, :HD] + both[:, HD:]
+
+    def relay_last():
+        acopy[2, "R", 0].wait_recv()
+        acopy[2, "RR"] = send(ab.at[2, 1, top], ab.at[2, 3, top], ars.at[2, 4], at_x(1))
+        acopy[2, "L", 1].wait_recv()
+        acopy[2, "LL"] = send(ab.at[2, 2, low], ab.at[2, 3, low], ars.at[2, 5], at_x(3))
+
+    def send_checks():
+        csb[g] = (csp[...] * D ** (-0.5)).T[0:8]
+        for k in range(1, 8):
+            send(csb.at[g], csb.at[g], crs.at[k], (f, (g + k) % 8))
 
     def relay_a(h):
         relay_ring(ab, acopy, ars, at_x, h)
@@ -391,12 +423,11 @@
     def arrived_a(h):
         arrived_ring(acopy, h)
 
-    def last_rows(pair, side):
-        rows = jnp.concatenate([ab[2, pair], ab[2, pair + 1]], axis=1)
-        block = jnp.concatenate(
-            [wx[pair, side, 2 * HD : COLS, :], wx[pair + 1, side, 2 * HD : COLS, :]], axis=0
-        )
-        return jnp.dot(rows, block, preferred_element_type=F32)
+    def last_rows(half, side):
+        part = slice(half * BLK, (half + 1) * BLK)
+        rows = jnp.concatenate([ab[2, k, part, :] for k in range(4)], axis=1)
+        block = jnp.concatenate([wx[k, side, 2 * HD : COLS, :] for k in range(4)], axis=0)
+        return po[side, part, :] + jnp.dot(rows, block, preferred_element_type=F32)
 
     def project_first():
         for side in range(2):
@@ -407,23 +438,7 @@
                 total = part if total is None else total + part
             po[side] = total
 
-    def project_near():
-        for side in range(2):
-            po[side] = po[side] + last_rows(0, side)
-
-    def finish():
-        other = (c + zl + 1) % 2
-        given = po[other] + last_rows(2, other)
-        zs[...] = given.astype(BF)
-        zcopy = send(zs, zr, zrs.at[0], zlo)
-        kept = po[1 - other] + last_rows(2, 1 - other)
-        sums = given + kept
-        turned = (sums[:, :HD] + sums[:, HD : 2 * HD] + sums[:, 2 * HD :]).T
-        total = jnp.sum(turned, axis=0, keepdims=True) * D ** (-0.5)
-        csb[g] = jnp.broadcast_to(total, (8, SLAB))
-        for k in range(1, 8):
-            send(csb.at[g], csb.at[g], crs.at[k], (f, (g + k) % 8))
-        po[0] = kept
+    def close_checks():
         for k in range(1, 8):
             pltpu.make_async_remote_copy(
                 src_ref=csb.at[(g + 8 - k) % 8],
@@ -437,12 +452,30 @@
         for k in range(1, 8):
             checks = checks + csb[k]
         cs_ref[...] = checks[0]
-        zcopy.wait_recv()
-        out_ref[...] = (po[0] + zr[...].astype(F32)).astype(BF)
 
     def drain(count):
         for i in range(count):
             sent(i)
+
+    def finish():
+        other = (c + zl + 1) % 2
+        zcopy = []
+        for half in range(2):
+            if half == 0:
+                acopy[2, "L", 0].wait_recv()
+                acopy[2, "RR"].wait_recv()
+            else:
+                acopy[2, "R", 1].wait_recv()
+                acopy[2, "LL"].wait_recv()
+            part = (top, low)[half]
+            zs[part, :] = last_rows(half, other).astype(BF)
+            zcopy.append(send(zs.at[part], zr.at[part], zrs.at[half], zlo))
+        kept = [last_rows(half, 1 - other) for half in range(2)]
+        drain(len(started) - 2)
+        for half in range(2):
+            rows = slice(half * BLK, (half + 1) * BLK)
+            zcopy[half].wait_recv()
+            out_ref[rows, :] = (kept[half] + zr[rows, :].astype(F32)).astype(BF)
 
     make_first()
     pl.semaphore_wait(barrier, len(peers))
@@ -452,58 +485,59 @@
     send_q(0)
     make_rest()
     send_q(1)
+    send_q(2)
     make_kv(1)
     send_kv(1)
+    make_kv(2)
     for copy in wx_in:
         copy.wait()
-    make_kv(2)
     send_w()
     relay_t()
     relay_kv(0)
     send_kv(2)
+    row_sums()
+    last_kv(0)
+    relay_kv(1)
     relay_q(0)
-    send_q(2)
-    relay_kv(1)
-    last_kv(0)
     relay_q(1)
     limits_table()
     arrived_kv(0)
     attend_sides(0)
     relay_kv(2)
+    relay_q(2)
+    last_kv(1)
     arrived_q(0)
     attend_opp(0)
-    last_kv(1)
-    relay_q(2)
     early = len(started)
     arrived_kv(1)
     attend_sides(1)
     last_kv(2)
     arrived_q(1)
     attend_opp(1)
+    relay_o(0)
     arrived_kv(2)
     arrived_q(2)
     attend_opp(2)
+    attend_own(0)
     attend_sides(2)
-    relay_o(0)
+    relay_o(1)
     share_w()
-    attend_own(0)
-    relay_o(1)
     attend_own(1)
     attend_own(2)
+    combine(0)
     relay_o(2)
     drain(early)
     arrived_w()
-    combine(0)
     combine(1)
     relay_a(0)
     combine(2)
+    send_checks()
     relay_a(1)
-    relay_a(2)
+    relay_last()
     arrived_a(0)
     arrived_a(1)
     project_first()
-    project_near()
-    arrived_a(2)
+    close_checks()
     finish()
     drain(len(started))
 
@@ -537,6 +571,9 @@
             pltpu.VMEM((HL, D, 2 * HD), BF),
             pltpu.VMEM((D, COLS), BF),
             pltpu.VMEM((4, 2, COLS, COLS), BF),
+            pltpu.VMEM((COLS, D), BF),
+            pltpu.VMEM((COLS, 2 * HD), BF),
+            pltpu.VMEM((SLAB, HD), F32),
             pltpu.VMEM((HL, 8, SLAB, 2 * HD), BF),
             pltpu.VMEM((HL, 4, SLAB, HD), BF),
             pltpu.VMEM((2, COLS), F32),
@@ -565,8 +602,8 @@
             dma((3,)),
             dma((7,)),
             dma((HL, 6)),
-            dma((HL, 4)),
-            dma((1,)),
+            dma((HL, 6)),
+            dma((2,)),
             dma((8,)),
         ],
         compiler_params=pltpu.CompilerParams(

time: 60.3 us -> 55.9 us (0.927)
  Pallas kernels: 59.5 us -> 55 us
    pallas_call x1, Pallas kernels: 58.8 us -> 54.3 us  [per_device(): pl.pallas_call(layer_kernel, name='layer', out_shape=(pltpu.VMEM((SLAB, C...]
where the time goes in v4:
time: 55.9 us; the launch traced here: 55.8 us
  Pallas kernels  55 us (98%)
  between operations  0.8 us (1%)
    pallas_call x1, Pallas kernels, per_device(): pl.pallas_call(layer_kernel, name='layer', out_shape=(pltpu.VMEM((SLAB, C...  54.3 us

profile of v4, /device:TPU:2, one launch (start us, length us, event | category | flops | bytes accessed | tf_op | source)
XLA Modules:
  0.0 55.8 jit_solution(16056964762572002880)
XLA Ops:
  0.6 54.3 %layer.1 = (bf16[256,384]{1,0:T(8,128)(2,1)S(1)}, f32[256]{0:T(256)S(1)}) custom-call(bf16[256,3072]{1,0:T(8,128)(2,1)} %tok_hbm.1, bf16[3,3072,384]{2,1,0:T(8,128)(2,1)} %w_hbm.1, bf16[384,3072]{1,0:T(8,128)(2,1)} %wo_hbm.1, f32[2,384]{1,0:T(2,128)} %gains_hbm.1, s32[2,4]{1,0:T(2,128)} %near_hbm.1, s32[2,64]{1,0:T(2,128)} %far_hbm.1, s32[32]{0:T(128)} %window_hbm.1), custom_call_target="tpu_custom_call" | custom-call | tf_op jit(solution)/shard_map/layer/pallas_call | solution.py:560
  55.0 0.7 %place.1 = (bf16[256,384]{1,0:T(8,128)(2,1)}, f32[256]{0:T(256)}) custom-call(bf16[256,384]{1,0:T(8,128)(2,1)S(1)} %get-tuple-element.4.rows_ref, f32[256]{0:T(256)S(1)} %get-tuple-element.5.sums_ref), custom_call_target="tpu_custom_call" | custom-call | tf_op jit(solution)/shard_map/place/pallas_call | solution.py:613

commit v5 on v4

--- a/solution.py
+++ b/solution.py
@@ -21,7 +21,16 @@
 NT = (((1,), (1,)), ((), ()))
 
 
-def layer_kernel(
+def layer_body(
+    pool,
+    krs,
+    qrs,
+    trs,
+    wrs,
+    ors,
+    ars,
+    zrs,
+    crs,
     tok_hbm,
     w_hbm,
     wo_hbm,
@@ -60,15 +69,6 @@
     zs,
     zr,
     csb,
-    pool,
-    krs,
-    qrs,
-    trs,
-    wrs,
-    ors,
-    ars,
-    zrs,
-    crs,
 ):
     f = lax.axis_index("frame")
     g = lax.axis_index("head")
@@ -119,12 +119,6 @@
     def columns(side, step):
         at = (side * 4 + (x + step) % 4) * COLS
         return pl.ds(pl.multiple_of(at, HD), COLS)
-
-    barrier = pltpu.get_barrier_semaphore()
-    peers = [at_y(1), at_y(3), core, at_z(1), at_z(3)]
-    peers += [(f, (g + k) % 8) for k in range(1, 8)]
-    for peer in peers:
-        pl.semaphore_signal(barrier, inc=1, device_id=peer, device_id_type=MESH)
 
     small_in = [
         fetch(near_hbm, near_ref, 10),
@@ -142,6 +136,12 @@
                 fetch(w_hbm.at[2, span, pl.ds(0, HD)], wkv.at[0, span, pl.ds(HD, HD)], 3 * k + 2),
             )
         )
+    barrier = pltpu.get_barrier_semaphore()
+    peers = [at_y(1), at_y(3), core, at_z(1), at_z(3)]
+    peers += [(f, (g + k) % 8) for k in range(1, 8)]
+    for peer in peers:
+        pl.semaphore_signal(barrier, inc=1, device_id=peer, device_id_type=MESH)
+
     first, rest = pl.ds(0, HD), pl.ds(HD, 2 * HD)
     q_first = fetch(w_hbm.at[0, :, first], wq.at[:, first], 14)
     q_rest = fetch(w_hbm.at[0, :, rest], wq.at[:, rest], 15)
@@ -542,6 +542,12 @@
     drain(len(started))
 
 
+def layer_kernel(*refs):
+    dma = pltpu.SemaphoreType.DMA
+    shapes = ((POOL,), (HL, 8), (HL, 4), (3,), (7,), (HL, 6), (HL, 6), (2,), (8,))
+    pl.run_scoped(lambda *sems: layer_body(*sems, *refs), *(dma(shape) for shape in shapes))
+
+
 def place_kernel(rows_ref, sums_ref, rows_hbm, sums_hbm, sem):
     copies = [
         pltpu.make_async_copy(rows_ref, rows_hbm, sem.at[0]),
@@ -596,15 +602,6 @@
             pltpu.VMEM((SLAB, COLS), BF),
             pltpu.VMEM((SLAB, COLS), BF),
             pltpu.VMEM((8, 8, SLAB), F32),
-            dma((POOL,)),
-            dma((HL, 8)),
-            dma((HL, 4)),
-            dma((3,)),
-            dma((7,)),
-            dma((HL, 6)),
-            dma((HL, 6)),
-            dma((2,)),
-            dma((8,)),
         ],
         compiler_params=pltpu.CompilerParams(
             collective_id=0, has_side_effects=True, vmem_limit_bytes=56 * 1024 * 1024

time: 55.9 us -> 54.3 us (0.971)
  Pallas kernels: 55 us -> 53.4 us
    pallas_call x1, Pallas kernels: 54.3 us -> 52.7 us  [per_device(): pl.pallas_call(layer_kernel, name='layer', out_shape=(pltpu.VMEM((SLAB, C...]
where the time goes in v5:
time: 54.3 us; the launch traced here: 54.2 us
  Pallas kernels  53.4 us (98%)
  between operations  0.8 us (1%)
    pallas_call x1, Pallas kernels, per_device(): pl.pallas_call(layer_kernel, name='layer', out_shape=(pltpu.VMEM((SLAB, C...  52.7 us

profile of v5, /device:TPU:2, one launch (start us, length us, event | category | flops | bytes accessed | tf_op | source)
XLA Modules:
  0.0 54.2 jit_solution(13752947117408815172)
XLA Ops:
  0.6 52.7 %layer.1 = (bf16[256,384]{1,0:T(8,128)(2,1)S(1)}, f32[256]{0:T(256)S(1)}) custom-call(bf16[256,3072]{1,0:T(8,128)(2,1)} %refs_0_.1, bf16[3,3072,384]{2,1,0:T(8,128)(2,1)} %refs_1_.1, bf16[384,3072]{1,0:T(8,128)(2,1)} %refs_2_.1, f32[2,384]{1,0:T(2,128)} %refs_3_.1, s32[2,4]{1,0:T(2,128)} %refs_4_.1, s32[2,64]{1,0:T(2,128)} %refs_5_.1, s32[32]{0:T(128)} %refs_6_.1), custom_call_target="tpu_custom_call" | custom-call | tf_op jit(solution)/shard_map/layer/pallas_call | solution.py:566
  53.3 0.7 %place.1 = (bf16[256,384]{1,0:T(8,128)(2,1)}, f32[256]{0:T(256)}) custom-call(bf16[256,384]{1,0:T(8,128)(2,1)S(1)} %get-tuple-element.4.rows_ref, f32[256]{0:T(256)S(1)} %get-tuple-element.5.sums_ref), custom_call_target="tpu_custom_call" | custom-call | tf_op jit(solution)/shard_map/place/pallas_call | solution.py:610

commit v6 on v5

--- a/solution.py
+++ b/solution.py
@@ -429,14 +429,13 @@
         block = jnp.concatenate([wx[k, side, 2 * HD : COLS, :] for k in range(4)], axis=0)
         return po[side, part, :] + jnp.dot(rows, block, preferred_element_type=F32)
 
-    def project_first():
+    def project(h):
+        span = slice(h * HD, (h + 1) * HD)
+        rows = jnp.concatenate([ab[h, k] for k in range(4)], axis=1)
         for side in range(2):
-            total = None
-            for k in range(4):
-                rows = jnp.concatenate([ab[0, k], ab[1, k]], axis=1)
-                part = jnp.dot(rows, wx[k, side, 0 : 2 * HD, :], preferred_element_type=F32)
-                total = part if total is None else total + part
-            po[side] = total
+            block = jnp.concatenate([wx[k, side, span, :] for k in range(4)], axis=0)
+            part = jnp.dot(rows, block, preferred_element_type=F32)
+            po[side] = part if h == 0 else po[side] + part
 
     def close_checks():
         for k in range(1, 8):
@@ -535,8 +534,9 @@
     relay_a(1)
     relay_last()
     arrived_a(0)
+    project(0)
     arrived_a(1)
-    project_first()
+    project(1)
     close_checks()
     finish()
     drain(len(started))

time: 54.3 us -> 54.3 us (level)
  no operation moved by 1% of the time
where the time goes in v6:
time: 54.3 us; the launch traced here: 54.2 us
  Pallas kernels  53.4 us (98%)
  between operations  0.8 us (1%)
    pallas_call x1, Pallas kernels, per_device(): pl.pallas_call(layer_kernel, name='layer', out_shape=(pltpu.VMEM((SLAB, C...  52.7 us

profile of v6, /device:TPU:2, one launch (start us, length us, event | category | flops | bytes accessed | tf_op | source)
XLA Modules:
  0.0 54.2 jit_solution(7768848070902715830)
XLA Ops:
  0.6 52.7 %layer.1 = (bf16[256,384]{1,0:T(8,128)(2,1)S(1)}, f32[256]{0:T(256)S(1)}) custom-call(bf16[256,3072]{1,0:T(8,128)(2,1)} %refs_0_.1, bf16[3,3072,384]{2,1,0:T(8,128)(2,1)} %refs_1_.1, bf16[384,3072]{1,0:T(8,128)(2,1)} %refs_2_.1, f32[2,384]{1,0:T(2,128)} %refs_3_.1, s32[2,4]{1,0:T(2,128)} %refs_4_.1, s32[2,64]{1,0:T(2,128)} %refs_5_.1, s32[32]{0:T(128)} %refs_6_.1), custom_call_target="tpu_custom_call" | custom-call | tf_op jit(solution)/shard_map/layer/pallas_call | solution.py:566
  53.3 0.7 %place.1 = (bf16[256,384]{1,0:T(8,128)(2,1)}, f32[256]{0:T(256)}) custom-call(bf16[256,384]{1,0:T(8,128)(2,1)S(1)} %get-tuple-element.4.rows_ref, f32[256]{0:T(256)S(1)} %get-tuple-element.5.sums_ref), custom_call_target="tpu_custom_call" | custom-call | tf_op jit(solution)/shard_map/place/pallas_call | solution.py:610
